TPU v7x, 256 devices: a whole 4x4x8 slice. The times are simulated.
256 devices in a mesh: chaos: 64 (over z, y, core), mesh: 4 (over x).
Axes of the slice: x: 4, y: 4, z: 8, core: 2. Of those that a mesh axis runs over, the one named last changes fastest.
Arguments:
- coefficients: bfloat16 [128, 96, 320], P('mesh', None, 'chaos'), may hold values from -6 to 6
- stiffness: bfloat16 [11, 12288, 6, 96], P(None, ('mesh', 'chaos')), may hold values from -0.25 to 0.25
- columns: int32 [128, 6], P('mesh'), may hold values from 0 to 127
- pair_rows: int32 [11, 1280], replicated, may hold values from 0 to 319
- pair_cols: int32 [11, 1280], replicated, may hold values from 0 to 319
- pair_vals: float32 [11, 1280], replicated, may hold values from -2 to 2
Outputs:
- applied: bfloat16 [128, 96, 320], P('mesh', None, 'chaos')
All inputs are finite; a program needn't handle non-finite values.
Results may differ from a plain program's by a relative error of at most 0.001.
Values may be sent and summed in bfloat16 or wider, within the bound.
No kernel may reach another device: no remote copies, remote signals or barrier semaphores. Data moves between devices by JAX's collectives and lax.ppermute only.
A program may use at most 128 MiB of HBM per device.

v0:
```python
import jax
import jax.numpy as jnp
from jax import lax
from jax.sharding import PartitionSpec as P


def from_everyone(shard, axis):
    devices = lax.axis_size(axis)
    return lax.all_to_all(
        jnp.broadcast_to(shard[None], (devices, *shard.shape)), axis, 0, 0, tiled=True
    )


def joined_along(blocks, dim):
    blocks = jnp.moveaxis(blocks, 0, dim)
    lengths = blocks.shape
    return blocks.reshape(*lengths[:dim], lengths[dim] * lengths[dim + 1], *lengths[dim + 2 :])


def collect(shard, axis, dim):
    blocks = from_everyone(shard, axis)
    return joined_along(blocks, dim)


def indicator(indices, count):
    targets = lax.iota(jnp.int32, count)
    return (indices[:, :, None] == targets[None, None, :]).astype(jnp.float32)


def local(coefficients, stiffness, columns, pair_rows, pair_cols, pair_vals):
    whole_nodes = collect(coefficients, "mesh", 0)
    own_count = coefficients.shape[2]
    node_count = coefficients.shape[0]
    block_size = coefficients.shape[1]
    chaos_count = lax.axis_size("chaos")
    total_count = own_count * chaos_count
    row_count = stiffness.shape[1]
    row_first = lax.axis_index("chaos") * row_count
    row_nodes = (row_first + lax.iota(jnp.int32, row_count)) // block_size
    span = (row_count - 1) // block_size + 2
    peer_first = lax.iota(jnp.int32, chaos_count) * row_count // block_size
    peer_nodes = jnp.minimum(
        peer_first[:, None] + lax.iota(jnp.int32, span)[None, :], node_count - 1
    )
    outgoing = whole_nodes[columns[peer_nodes.reshape(-1)]]
    received = lax.all_to_all(outgoing, "chaos", split_axis=0, concat_axis=3, tiled=True)
    local_index = row_nodes - row_first // block_size
    picked = received[local_index]
    products = jnp.einsum("krsb,rsbj->krj", stiffness, picked, preferred_element_type=jnp.float32)
    weighted = indicator(pair_cols, total_count) * pair_vals[:, :, None]
    every_row = indicator(pair_rows, total_count)
    coupling = jnp.einsum("klj,kli->kji", weighted, every_row, precision=lax.Precision.HIGHEST)
    finished = jnp.einsum(
        "krj,kji->ri", products, coupling, precision=lax.Precision.HIGHEST
    ).astype(jnp.bfloat16)
    returned = lax.all_to_all(finished, "chaos", split_axis=1, concat_axis=0, tiled=True)
    return returned.reshape(node_count, block_size, own_count)


def solution(mesh):
    return jax.shard_map(
        local,
        mesh=mesh,
        in_specs=(
            P("mesh", None, "chaos"),
            P(None, ("mesh", "chaos"), None, None),
            P("mesh", None),
            P(),
            P(),
            P(),
        ),
        out_specs=P("mesh", None, "chaos"),
        check_vma=False,
    )
```

profile of v0, /device:TPU:1, one launch (start us, length us, event | category | flops | bytes accessed | tf_op | source)
XLA Modules:
  0.0 106.6 jit_solution(10954965246318827999)
XLA Ops:
  0.0 1.5 %broadcast_in_dim.2 = bf16[4,32,96,5]{2,1,3,0:T(8,128)(2,1)} broadcast(bf16[32,96,5]{1,0,2:T(8,128)(2,1)} %param.6), dimensions={1,2,3} | broadcast | bytes 153600 | tf_op jit(solution)/shard_map/broadcast_in_dim | solution.py:10
  1.5 4.8 %all-to-all-start = ((bf16[4,32,96,5]{2,1,3,0:T(8,128)(2,1)}), bf16[4,32,96,5]{2,1,3,0:T(8,128)(2,1)S(1)}, u32[]{:S(2)}, u32[]{:S(2)}) async-start(bf16[4,32,96,5]{2,1,3,0:T(8,128)(2,1)} %broadcast_in_dim.2), calls=%async_computation | async-start | bytes 327680 | tf_op jit(solution)/shard_map/all_to_all | solution.py:9
  6.4 0.1 add_minimum_fusion
  6.5 0.1 min.19
  6.6 0.8 copy.42
  7.4 0.6 gather_fusion
  8.1 0.1 reshape.129
  8.2 3.2 %all-to-all-done = bf16[4,32,96,5]{2,1,3,0:T(8,128)(2,1)S(1)} async-done(((bf16[4,32,96,5]{2,1,3,0:T(8,128)(2,1)}), bf16[4,32,96,5]{2,1,3,0:T(8,128)(2,1)S(1)}, u32[]{:S(2)}, u32[]{:S(2)}) %all-to-all-start) | async-done | bytes 122912 | tf_op jit(solution)/shard_map/all_to_all | solution.py:9
  11.4 0.1 copy.41
  11.5 2.4 %gather_fusion.1 = bf16[768,96,5]{1,2,0:T(8,128)(2,1)S(1)} fusion(bf16[128,96,5]{1,2,0:T(8,128)(2,1)S(1)} %bitcast.30, s32[1024]{0:T(1024)S(1)} %pad_clamp_fusion.1), kind=kCustom, calls=%fused_computation.1 | custom fusion | bytes 1477632 | tf_op jit(solution)/shard_map/gather | solution.py:45
  13.9 1.3 %copy.44 = bf16[128,6,96,5]{2,1,3,0:T(8,128)(2,1)} copy(bf16[128,6,96,5]{2,3,1,0:T(8,128)(2,1)S(1)} %bitcast.31) | data formatting | bytes 1474560 | tf_op jit(solution)/shard_map/gather | solution.py:45
  15.3 13.8 %all-to-all-start.1 = ((bf16[128,6,96,5]{2,1,3,0:T(8,128)(2,1)}), bf16[128,6,96,5]{2,1,3,0:T(8,128)(2,1)S(1)}, u32[]{:S(2)}, u32[]{:S(2)}) async-start(bf16[128,6,96,5]{2,1,3,0:T(8,128)(2,1)} %copy.44), calls=%async_computation.1 | async-start | bytes 2621440 | tf_op jit(solution)/shard_map/all_to_all | solution.py:46
  29.1 26.0 %fusion = f32[11,320,320]{2,1,0:T(8,128)} fusion(s32[11,1280]{1,0:T(8,128)S(1)} %copy-done.1, f32[11,1280]{1,0:T(8,128)S(1)} %copy-done.2, s32[11,1280]{1,0:T(8,128)S(1)} %copy-done.3), kind=kOutput, calls=%fused_computation.4 | convolution fusion | flops 17315020800 | bytes 4674560 | tf_op jit(solution)/shard_map/klj,kli->kji/dot_general | solution.py:52
  55.1 7.5 %all-to-all-done.1 = bf16[128,6,96,5]{2,1,3,0:T(8,128)(2,1)S(1)} async-done(((bf16[128,6,96,5]{2,1,3,0:T(8,128)(2,1)}), bf16[128,6,96,5]{2,1,3,0:T(8,128)(2,1)S(1)}, u32[]{:S(2)}, u32[]{:S(2)}) %all-to-all-start.1) | async-done | bytes 737312 | tf_op jit(solution)/shard_map/all_to_all | solution.py:46
  62.7 0.2 copy.45
  62.9 0.7 copy.46
  63.6 1.1 %copy.47 = bf16[2,6,96,320]{3,2,1,0:T(8,128)(2,1)S(1)} copy(bf16[2,6,96,320]{2,0,3,1:T(2,128)(2,1)S(1)} %bitcast.32) | data formatting | bytes 1474560 | tf_op jit(solution)/shard_map/all_to_all | solution.py:46
  64.7 9.2 %gather_fusion.2 = bf16[48,6,96,320]{3,2,1,0:T(8,128)(2,1)} fusion(bf16[2,6,96,320]{3,2,1,0:T(8,128)(2,1)S(1)} %copy.47, s32[1024]{0:T(1024)S(1)} %pad_clamp_fusion), kind=kCustom, calls=%fused_computation.2 | custom fusion | bytes 35389632 | tf_op jit(solution)/shard_map/gather | solution.py:48
  73.9 8.8 %convolution_bitcast_fusion = f32[11,48,320]{2,0,1:T(8,128)S(1)} fusion(bf16[48,6,96,320]{3,2,1,0:T(8,128)(2,1)} %gather_fusion.2, bf16[11,48,6,96]{3,1,2,0:T(8,128)(2,1)S(1)} %copy-done), kind=kOutput, calls=%fused_computation.11 | convolution fusion | flops 194641920 | bytes 18978816 | tf_op jit(solution)/shard_map/krsb,rsbj->krj/dot_general | solution.py:49
  82.7 5.8 %fusion.7 = bf16[48,320]{1,0:T(8,128)(2,1)S(1)} fusion(f32[11,320,320]{2,1,0:T(8,128)} %fusion, f32[11,48,320]{2,0,1:T(8,128)S(1)} %convolution_bitcast_fusion), kind=kOutput, calls=%fused_computation.14 | convolution fusion | flops 648821760 | bytes 5212160 | tf_op jit(solution)/shard_map/krj,kji->ri/dot_general | solution.py:53
  88.5 0.1 copy.50
  88.6 0.1 all_to_all.33
  88.7 17.2 %all_to_all.39 = bf16[48,64,5]{0,2,1:T(8,128)(2,1)S(1)} all-to-all(bf16[48,64,5]{0,2,1:T(8,128)(2,1)S(1)} %all_to_all.33), channel_id=1, replica_groups=mesh['chaos'=64,'mesh'=4] {'chaos'}, dimensions={1} | all-to-all | bytes 61440 | tf_op jit(solution)/shard_map/all_to_all | solution.py:56
  105.9 0.7 reshape.118
  (16 shorter events, 0.1 us)
Async XLA Ops:
  0.0 73.9 %copy-start = (bf16[11,48,6,96]{3,1,2,0:T(8,128)(2,1)S(1)}, bf16[11,48,6,96]{3,1,2,0:T(8,128)(2,1)}, u32[]{:S(2)}) copy-start(bf16[11,48,6,96]{3,1,2,0:T(8,128)(2,1)} %param.7) | copy-start | bytes 1824772
  1.5 9.8 %all-to-all-start = ((bf16[4,32,96,5]{2,1,3,0:T(8,128)(2,1)}), bf16[4,32,96,5]{2,1,3,0:T(8,128)(2,1)S(1)}, u32[]{:S(2)}, u32[]{:S(2)}) async-start(bf16[4,32,96,5]{2,1,3,0:T(8,128)(2,1)} %broadcast_in_dim.2), calls=%async_computation | async-start | bytes 327680 | tf_op jit(solution)/shard_map/all_to_all | solution.py:9
  13.9 15.2 %copy-start.1 = (s32[11,1280]{1,0:T(8,128)S(1)}, s32[11,1280]{1,0:T(8,128)}, u32[]{:S(2)}) copy-start(s32[11,1280]{1,0:T(8,128)} %param.9) | copy-start | bytes 168964
  13.9 15.2 %copy-start.2 = (f32[11,1280]{1,0:T(8,128)S(1)}, f32[11,1280]{1,0:T(8,128)}, u32[]{:S(2)}) copy-start(f32[11,1280]{1,0:T(8,128)} %param.11) | copy-start | bytes 168964
  13.9 15.2 %copy-start.3 = (s32[11,1280]{1,0:T(8,128)S(1)}, s32[11,1280]{1,0:T(8,128)}, u32[]{:S(2)}) copy-start(s32[11,1280]{1,0:T(8,128)} %param.10) | copy-start | bytes 168964
  15.3 47.4 %all-to-all-start.1 = ((bf16[128,6,96,5]{2,1,3,0:T(8,128)(2,1)}), bf16[128,6,96,5]{2,1,3,0:T(8,128)(2,1)S(1)}, u32[]{:S(2)}, u32[]{:S(2)}) async-start(bf16[128,6,96,5]{2,1,3,0:T(8,128)(2,1)} %copy.44), calls=%async_computation.1 | async-start | bytes 2621440 | tf_op jit(solution)/shard_map/all_to_all | solution.py:46
where the time goes:
time: 107 us
  matrix products  40.6 us (38%)
  local copies, waits for them, and re-layouts  19.2 us (18%)
  starting transfers between devices  18.6 us (17%)
  blocking collectives  17.2 us (16%)
  waiting for transfers between devices  10.7 us (10%)
    dot_general x1, matrix products, local(): jnp.einsum('klj,kli->kji', weighted, every_row, precision=lax.Precision.H...  26 us
    all_to_all x1, blocking collectives, local(): lax.all_to_all(finished, 'chaos', split_axis=1, concat_axis=0, tiled=True)  17.2 us
    all_to_all x1, starting transfers between devices, local(): lax.all_to_all(outgoing, 'chaos', split_axis=0, concat_axis=3, tiled=True)  13.8 us
    gather x1, local copies, waits for them, and re-layouts, local(): picked = received[local_index]  9.2 us
    dot_general x1, matrix products, local(): jnp.einsum('krsb,rsbj->krj', stiffness, picked, preferred_element_type=jn...  8.8 us
    all_to_all x1, waiting for transfers between devices, local(): lax.all_to_all(outgoing, 'chaos', split_axis=0, concat_axis=3, tiled=True)  7.53 us
    dot_general x1, matrix products, local(): jnp.einsum('krj,kji->ri', products, coupling, precision=lax.Precision.HIG...  5.76 us
    all_to_all x1, starting transfers between devices, from_everyone(): lax.all_to_all(jnp.broadcast_to(shard[None], (devices, *shard.shape)), ax...  4.83 us
  transfers between devices with their start and end apart: 2, of which 2 were waited for; matrix products, arithmetic and copies ran while one was open for 26% of the time, Pallas kernels for 0%

commit v1 on v0

v1 whole, which is shorter than its diff:
```python
import jax
import jax.numpy as jnp
from jax import lax
from jax.experimental import pallas as pl
from jax.experimental.pallas import tpu as pltpu
from jax.sharding import Mesh, PartitionSpec as P

LANES = 128
BF16 = jnp.bfloat16
F32 = jnp.float32


def split_two(value):
    high = value.astype(BF16)
    return high, (value - high.astype(F32)).astype(BF16)


def call(body, name, outs, scratch=(), **specs):
    return pl.pallas_call(
        body,
        out_shape=outs,
        scratch_shapes=scratch,
        compiler_params=pltpu.CompilerParams(vmem_limit_bytes=40 << 20),
        name=name,
        **specs,
    )


def coupling_kernel(own, parts, rows_ref, cols_ref, vals_ref, high_ref, low_ref, total_ref):
    modes, pairs = rows_ref.shape
    half = own * parts
    total_ref[...] = jnp.zeros_like(total_ref)
    out_iota = lax.broadcasted_iota(jnp.int32, (2 * half, pairs), 0)
    in_iota = lax.broadcasted_iota(jnp.int32, (2 * LANES, pairs), 0)
    for mode in range(modes):
        first = mode * half
        base = first // LANES * LANES
        rows = rows_ref[mode : mode + 1, :]
        cols = cols_ref[mode : mode + 1, :] + (first - base)
        vals = vals_ref[mode : mode + 1, :]
        high, low = split_two(vals)
        every_row = jnp.where(out_iota == rows, 1.0, 0.0).astype(BF16)
        hit = in_iota == cols
        w_high = jnp.where(hit, high.astype(F32), 0.0).astype(BF16)
        w_low = jnp.where(hit, low.astype(F32), 0.0).astype(BF16)
        dims = (((1,), (1,)), ((), ()))
        got = lax.dot_general(every_row, w_high, dims, preferred_element_type=F32)
        got += lax.dot_general(every_row, w_low, dims, preferred_element_type=F32)
        total_ref[:, base : base + 2 * LANES] += got
    high_ref[...], low_ref[...] = split_two(total_ref[...])


def rows_kernel(core_ref, mine_ref, theirs_ref, out_ref):
    modes, slots, rows, block = mine_ref.shape
    core = core_ref[0]
    out_ref[...] = jnp.zeros_like(out_ref)
    for ref, at in ((mine_ref, core), (theirs_ref, 1 - core)):
        for mode in range(modes):
            for slot in range(slots):
                start = pl.multiple_of(at * rows, 16)
                out_ref[mode, pl.ds(start, rows), slot * LANES : slot * LANES + block] = ref[mode, slot]


def select_kernel(target_ref, out_ref):
    count, width = out_ref.shape
    lanes = lax.broadcasted_iota(jnp.int32, (count, width), 1)
    out_ref[...] = jnp.where(lanes == target_ref[...], 1.0, 0.0).astype(BF16)


def send_kernel(select_ref, a_ref, b_ref, c_ref, d_ref, out_ref):
    own, nodes, block = a_ref.shape
    held = jnp.concatenate(
        [ref[...].reshape(own * nodes, block) for ref in (a_ref, b_ref, c_ref, d_ref)], axis=0
    )
    got = jnp.dot(select_ref[...], held, preferred_element_type=F32).astype(BF16)
    out_ref[...] = jnp.zeros_like(out_ref)
    out_ref[:, :block] = got


def apply_kernel(own, slots, got_ref, rows_ref, high_ref, low_ref, mine_ref, theirs_ref, wide, slotted, stacked):
    parts, unit, _ = got_ref.shape
    modes = rows_ref.shape[0]
    half = own * parts
    wide[: parts * unit, :] = got_ref[...].reshape(parts * unit, LANES).astype(F32)
    wide[parts * unit :, :] = jnp.zeros((8, LANES), F32)
    for slot in range(slots):
        for part in range(parts):
            slotted[slot, pl.ds(own * part, 8), :] = wide[pl.ds(unit * part + own * slot, 8), :]
    held = jnp.concatenate([slotted[slot, :half, :].astype(BF16) for slot in range(slots)], axis=1)
    products = lax.dot_general(
        held, rows_ref[...].reshape(modes * LANES, slots * LANES), (((1,), (1,)), ((), ())), preferred_element_type=F32
    )
    stacked[:, modes * half :, :] = jnp.zeros_like(stacked[:, modes * half :, :])
    for mode in range(modes):
        high, low = split_two(products[:, mode * LANES : (mode + 1) * LANES])
        stacked[0, mode * half : (mode + 1) * half, :] = high
        stacked[1, mode * half : (mode + 1) * half, :] = low
    high = stacked[0]
    total = jnp.dot(high_ref[...], high, preferred_element_type=F32)
    total += jnp.dot(high_ref[...], stacked[1], preferred_element_type=F32)
    total += jnp.dot(low_ref[...], high, preferred_element_type=F32)
    mine_ref[...] = total[:half]
    theirs_ref[...] = total[half:]


def finish_kernel(own, mine_ref, other_ref, out_ref, total):
    parts = out_ref.shape[0]
    half = own * parts
    total[:half, :] = mine_ref[...] + other_ref[...]
    total[half:, :] = jnp.zeros((8, LANES), F32)
    for part in range(parts):
        out_ref[part] = total[pl.ds(own * part, 8), :].astype(BF16)


def deliver_kernel(got_ref, out_ref, wide):
    own, nodes, block = out_ref.shape
    wide[...] = got_ref[...].reshape(nodes * 8, LANES).astype(F32)
    for i in range(own):
        out_ref[i] = wide[pl.ds(i, nodes, stride=8), :][:, :block].astype(BF16)


def local(coefficients, stiffness, columns, pair_rows, pair_cols, pair_vals):
    nodes, block, own = coefficients.shape
    modes, rows, slots, _ = stiffness.shape
    pairs = pair_rows.shape[1]
    parts = lax.axis_size("chip")
    meshes = lax.axis_size("mesh")
    half = own * parts
    unit = 32
    core = lax.axis_index("core")
    me = lax.axis_index("mesh")

    swap = [(0, 1), (1, 0)]
    mine = jnp.transpose(stiffness, (0, 2, 1, 3))
    theirs = lax.ppermute(mine, "core", swap)

    held = jnp.transpose(coefficients, (2, 0, 1))
    around = [held] + [
        lax.ppermute(held, "mesh", [(i, (i + d) % meshes) for i in range(meshes)]) for d in range(1, meshes)
    ]

    place = lax.rem(me - columns // nodes + meshes, meshes) * (own * nodes) + columns % nodes
    place = place[:, :, None] + (nodes * lax.iota(jnp.int32, own))[None, None, :]
    place = jnp.pad(place.reshape(parts, slots * own), ((0, 0), (0, unit - slots * own)), constant_values=-1)
    select = call(select_kernel, "select", jax.ShapeDtypeStruct((parts * unit, meshes * own * nodes), BF16))(
        place.reshape(parts * unit, 1)
    )
    outgoing = call(send_kernel, "send", jax.ShapeDtypeStruct((parts * unit, LANES), BF16))(select, *around)
    got = lax.all_to_all(outgoing.reshape(parts, unit, LANES), "chip", 0, 0, tiled=True)

    def share(index):
        part = index // (2 * own)
        rest = index - part * (2 * own)
        other = jnp.where(rest >= own, 1, 0)
        return part * own + rest - other * own, other

    row_at, row_core = share(pair_rows)
    col_at, col_core = share(pair_cols)
    row_at = row_at + jnp.where(row_core == core, 0, half)
    col_at = jnp.where(col_core == core, col_at, 4 * LANES)
    width = (modes * half + LANES - 1) // LANES * LANES
    high, low = call(
        lambda *refs: coupling_kernel(own, parts, *refs),
        "coupling",
        [jax.ShapeDtypeStruct((2 * half, width), BF16)] * 2,
        [pltpu.VMEM((2 * half, width), F32)],
    )(row_at, col_at, pair_vals)

    all_rows = call(
        rows_kernel,
        "rows",
        jax.ShapeDtypeStruct((modes, LANES, slots * LANES), BF16),
        in_specs=[pl.BlockSpec(memory_space=pltpu.SMEM)] + [pl.BlockSpec(memory_space=pltpu.VMEM)] * 2,
    )(core.reshape(1).astype(jnp.int32), mine, theirs)

    partial, other = call(
        lambda *refs: apply_kernel(own, slots, *refs),
        "apply",
        [jax.ShapeDtypeStruct((half, LANES), F32)] * 2,
        [
            pltpu.VMEM((parts * unit + 8, LANES), F32),
            pltpu.VMEM((slots, half + 8, LANES), F32),
            pltpu.VMEM((2, width, LANES), BF16),
        ],
    )(got, all_rows, high, low)
    other = lax.ppermute(other, "core", swap)
    finished = call(
        lambda *refs: finish_kernel(own, *refs),
        "finish",
        jax.ShapeDtypeStruct((parts, 8, LANES), BF16),
        [pltpu.VMEM((half + 8, LANES), F32)],
    )(partial, other)
    returned = lax.all_to_all(finished, "chip", 0, 0, tiled=True)
    out = call(
        deliver_kernel,
        "deliver",
        jax.ShapeDtypeStruct((own, nodes, block), BF16),
        [pltpu.VMEM((nodes * 8, LANES), F32)],
    )(returned)
    return jnp.transpose(out, (1, 2, 0))


def solution(mesh):
    chaos, meshes = mesh.devices.shape
    chips = Mesh(mesh.devices.reshape(chaos // 2, 2, meshes), ("chip", "core", "mesh"))
    spread = ("chip", "core")
    return jax.shard_map(
        local,
        mesh=chips,
        in_specs=(
            P("mesh", None, spread),
            P(None, ("mesh", *spread), None, None),
            P("mesh", None),
            P(),
            P(),
            P(),
        ),
        out_specs=P("mesh", None, spread),
        check_vma=False,
    )
```

time: 107 us -> 59.2 us (0.55)
  matrix products: 40.6 us -> 0 us
  local copies, waits for them, and re-layouts: 19.2 us -> 6.19 us
  Pallas kernels: 0 us -> 12.2 us
  waiting for transfers between devices: 10.7 us -> 1.42 us
  starting transfers between devices: 18.6 us -> 20 us
    dot_general x3 -> x0, matrix products: 40.6 us -> none  [the longest x1 26 us: local(): jnp.einsum('klj,kli->kji', weighted, every_row, precision=lax.Precision.H...]
    gather x4 -> x0, local copies, waits for them, and re-layouts: 13.6 us -> none  [the longest x1 9.2 us: local(): picked = received[local_index]]
    pallas_call x0 -> x7, Pallas kernels: none -> 12.2 us  [the longest x1 6.86 us: local(): call(lambda *refs: coupling_kernel(own, parts, *refs), 'coupling', [jax.S...]
    all_to_all x2 -> x1, waiting for transfers between devices: 10.7 us -> 0.01 us  [local(): lax.all_to_all(outgoing.reshape(parts, unit, LANES), 'chip', 0, 0, tiled=...]
    ppermute x0 -> x5, starting transfers between devices: none -> 8.47 us  [the longest x3 4.42 us: local(): lax.ppermute(held, 'mesh', [(i, (i + d) % meshes) for i in range(meshes)])]
    all_to_all x2 -> x1, starting transfers between devices: 18.6 us -> 11.5 us  [local(): lax.all_to_all(outgoing.reshape(parts, unit, LANES), 'chip', 0, 0, tiled=...]
    unnamed x9 -> x19, local copies, waits for them, and re-layouts: 0.79 us -> 5.55 us
    all_to_all x6 -> x0, local copies, waits for them, and re-layouts: 2.18 us -> none  [the longest x3 2.02 us: local(): lax.all_to_all(outgoing, 'chaos', split_axis=0, concat_axis=3, tiled=True)]
  transfers between devices with their start and end apart: 2 -> 6, of which waited for: 2 -> 3; matrix products, arithmetic and copies ran while one was open for 26% -> 3% of each run, Pallas kernels for 0% -> 13%
where the time goes in v1:
time: 59.2 us; the launch traced here: 58.8 us
  starting transfers between devices  20 us (34%)
  blocking collectives  17.9 us (30%)
  Pallas kernels  12.2 us (21%)
  local copies, waits for them, and re-layouts  6.19 us (10%)
  waiting for transfers between devices  1.42 us (2%)
  other arithmetic  0.95 us (2%)
    all_to_all x1, blocking collectives, local(): returned = lax.all_to_all(finished, 'chip', 0, 0, tiled=True)  17.9 us
    all_to_all x1, starting transfers between devices, local(): lax.all_to_all(outgoing.reshape(parts, unit, LANES), 'chip', 0, 0, tiled=...  11.5 us
    pallas_call x1, Pallas kernels, local(): call(lambda *refs: coupling_kernel(own, parts, *refs), 'coupling', [jax.S...  6.86 us
    unnamed x19, local copies, waits for them, and re-layouts  5.55 us
    ppermute x3, starting transfers between devices, local(): lax.ppermute(held, 'mesh', [(i, (i + d) % meshes) for i in range(meshes)])  4.42 us
    pallas_call x1, Pallas kernels, local(): call(lambda *refs: apply_kernel(own, slots, *refs), 'apply', [jax.ShapeDt...  2.77 us
    ppermute x1, starting transfers between devices, local(): other = lax.ppermute(other, 'core', swap)  2.54 us
    ppermute x1, starting transfers between devices, local(): theirs = lax.ppermute(mine, 'core', swap)  1.52 us
  transfers between devices with their start and end apart: 6, of which 3 were waited for; matrix products, arithmetic and copies ran while one was open for 3% of the time, Pallas kernels for 13%

profile of v1, /device:TPU:1, one launch (start us, length us, event | category | flops | bytes accessed | tf_op | source)
XLA Modules:
  0.0 58.8 jit_solution(17785932411191248764)
XLA Ops:
  0.0 3.3 %collective-permute-start.2 = (bf16[5,32,96]{2,1,0:T(8,128)(2,1)}, bf16[5,32,96]{2,1,0:T(8,128)(2,1)S(1)}, u32[]{:S(2)}, u32[]{:S(2)}) collective-permute-start(bf16[5,32,96]{2,1,0:T(8,128)(2,1)} %bitcast.9), channel_id=1, source_target_pairs={{0,3},{1,0},{2,1},{3,2},{4,7},{5,4},{6,5},{7,6},{8,11},{9,8},{10,9... | collective-permute-start | bytes 92168 | tf_op jit(solution)/shard_map/ppermute | solution.py:139
  3.3 0.5 collective-permute-start.1
  3.8 0.6 %collective-permute-start = (bf16[5,32,96]{2,1,0:T(8,128)(2,1)}, bf16[5,32,96]{2,1,0:T(8,128)(2,1)S(1)}, u32[]{:S(2)}, u32[]{:S(2)}) collective-permute-start(bf16[5,32,96]{2,1,0:T(8,128)(2,1)} %bitcast.11), channel_id=1, source_target_pairs={{0,1},{1,2},{2,3},{3,0},{4,5},{5,6},{6,7},{7,4},{8,9},{9,10},{10,1... | collective-permute-start | bytes 92168 | tf_op jit(solution)/shard_map/ppermute | solution.py:139
  4.4 1.5 %collective-permute-start.3 = (bf16[11,6,48,96]{3,2,1,0:T(8,128)(2,1)}, bf16[11,6,48,96]{3,2,1,0:T(8,128)(2,1)S(1)}, u32[]{:S(2)}, u32[]{:S(2)}) collective-permute-start(bf16[11,6,48,96]{3,2,1,0:T(8,128)(2,1)} %bitcast.7), channel_id=1, source_target_pairs={{0,4},{4,0},{1,5},{5,1},{2,6},{6,2},{3,7},{7,3},{8,12},{12,8},{9,1... | collective-permute-start | bytes 1824776 | tf_op jit(solution)/shard_map/ppermute | solution.py:135
  6.0 0.7 %fusion.10 = s32[32,6]{0,1:T(8,128)S(1)} fusion(s32[32,6]{0,1:T(8,128)} %param.8, s32[]{:T(128)S(6)} %axis_index.22), kind=kLoop, calls=%fused_computation.30 | loop fusion | flops 5568 | bytes 1540 | tf_op jit(solution)/shard_map/add | solution.py:142
  6.8 0.1 copy.10
  6.9 0.5 reshape.20.target_ref
  7.5 0.3 select.10.select_ref
  7.9 0.4 collective-permute-done.b_ref
  8.3 1.2 %send.1 = bf16[1024,128]{1,0:T(8,128)(2,1)} custom-call(bf16[1024,640]{1,0:T(8,128)(2,1)S(1)} %select.10.select_ref, bf16[5,32,96]{2,1,0:T(8,128)(2,1)S(1)} %bitcast.12, bf16[5,32,96]{2,1,0:T(8,128)(2,1)S(1)} %collective-permute-done.b_ref, bf16[5,32,96]{2,1,0:T(8,128)(2,1)S(1)} %collective-permute-done.1.c_ref, ...), custom_call_target="tpu_custom_call" | custom-call | tf_op jit(solution)/shard_map/send/pallas_call | solution.py:148
  9.5 11.5 %all-to-all-start = ((bf16[32,32,128]{2,1,0:T(8,128)(2,1)}), bf16[32,32,128]{2,1,0:T(8,128)(2,1)}, u32[]{:S(2)}, u32[]{:S(2)}) async-start(bf16[32,32,128]{2,1,0:T(8,128)(2,1)} %bitcast.1), calls=%async_computation | async-start | bytes 524288 | tf_op jit(solution)/shard_map/all_to_all | solution.py:149
  21.1 0.2 fusion.1
  21.2 6.9 %coupling.1 = (bf16[320,1792]{1,0:T(8,128)(2,1)S(1)}, bf16[320,1792]{1,0:T(8,128)(2,1)S(1)}) custom-call(s32[11,1280]{1,0:T(8,128)S(1)} %get-tuple-element.13.refs_0_, s32[11,1280]{1,0:T(8,128)S(1)} %get-tuple-element.14.refs_1_, f32[11,1280]{1,0:T(8,128)S(1)} %copy-done.5), custom_call_target="tpu_custom_call" | custom-call | tf_op jit(solution)/shard_map/coupling/pallas_call | solution.py:162
  28.1 1.0 %copy-done = bf16[320,1792]{1,0:T(8,128)(2,1)} copy-done((bf16[320,1792]{1,0:T(8,128)(2,1)}, bf16[320,1792]{1,0:T(8,128)(2,1)S(1)}, u32[]{:S(2)}) %copy-start) | copy-done | bytes 1146904
  29.1 0.9 %copy-done.3 = bf16[11,6,48,96]{3,2,1,0:T(8,128)(2,1)} copy-done((bf16[11,6,48,96]{3,2,1,0:T(8,128)(2,1)}, bf16[11,6,48,96]{3,2,1,0:T(8,128)(2,1)S(1)}, u32[]{:S(2)}) %copy-start.3) | copy-done | bytes 608280
  30.0 1.1 %copy-done.2 = bf16[11,48,6,96]{3,1,2,0:T(8,128)(2,1)S(1)} copy-done((bf16[11,48,6,96]{3,1,2,0:T(8,128)(2,1)S(1)}, bf16[11,48,6,96]{3,1,2,0:T(8,128)(2,1)}, u32[]{:S(2)}) %copy-start.2) | copy-done | bytes 608280
  31.2 1.1 %copy-done.4 = bf16[11,6,48,96]{3,2,1,0:T(8,128)(2,1)S(1)} copy-done((bf16[11,6,48,96]{3,2,1,0:T(8,128)(2,1)S(1)}, bf16[11,6,48,96]{3,2,1,0:T(8,128)(2,1)}, u32[]{:S(2)}) %copy-start.4) | copy-done | bytes 608280
  32.3 0.4 rows.1.refs_1_
  32.8 1.2 %copy-done.1 = bf16[320,1792]{1,0:T(8,128)(2,1)S(1)} copy-done((bf16[320,1792]{1,0:T(8,128)(2,1)S(1)}, bf16[320,1792]{1,0:T(8,128)(2,1)}, u32[]{:S(2)}) %copy-start.1) | copy-done | bytes 1146904
  34.0 2.8 %apply.1 = (f32[160,128]{1,0:T(8,128)S(1)}, f32[160,128]{1,0:T(8,128)S(1)}) custom-call(bf16[32,32,128]{2,1,0:T(8,128)(2,1)} %all-to-all-done.refs_0_, bf16[11,128,768]{2,1,0:T(8,128)(2,1)S(1)} %rows.1.refs_1_, bf16[320,1792]{1,0:T(8,128)(2,1)S(1)} %get-tuple-element.9.refs_2_, bf16[320,1792]{1,0:T(8,128)(2,1)S(1)} %copy-done.1), custom_call_target="tpu_custom_call" | custom-call | tf_op jit(solution)/shard_map/apply/pallas_call | solution.py:176
  36.8 2.5 %collective-permute-start.4 = (f32[160,128]{1,0:T(8,128)S(1)}, f32[160,128]{1,0:T(8,128)S(1)}, u32[]{:S(2)}, u32[]{:S(2)}) collective-permute-start(f32[160,128]{1,0:T(8,128)S(1)} %get-tuple-element.12), channel_id=1, source_target_pairs={{0,4},{4,0},{1,5},{5,1},{2,6},{6,2},{3,7},{7,3},{8,12},{12,8},{9,1... | collective-permute-start | bytes 245768 | tf_op jit(solution)/shard_map/ppermute | solution.py:186
  39.3 0.9 %collective-permute-done.4.refs_1_ = f32[160,128]{1,0:T(8,128)S(1)} collective-permute-done((f32[160,128]{1,0:T(8,128)S(1)}, f32[160,128]{1,0:T(8,128)S(1)}, u32[]{:S(2)}, u32[]{:S(2)}) %collective-permute-start.4) | collective-permute-done | bytes 81952 | tf_op jit(solution)/shard_map/ppermute | solution.py:186
  40.3 17.9 %all_to_all.10.got_ref = bf16[32,8,128]{2,1,0:T(8,128)(2,1)S(1)} all-to-all(bf16[32,8,128]{2,1,0:T(8,128)(2,1)S(1)} %finish.1), channel_id=1, replica_groups=mesh['chip'=32,'core'=2,'mesh'=4] {'chip'}, dimensions={0} | all-to-all | bytes 131072 | tf_op jit(solution)/shard_map/all_to_all | solution.py:193
  58.1 0.6 %deliver.1 = bf16[5,32,96]{2,1,0:T(8,128)(2,1)} custom-call(bf16[32,8,128]{2,1,0:T(8,128)(2,1)S(1)} %all_to_all.10.got_ref), custom_call_target="tpu_custom_call" | custom-call | tf_op jit(solution)/shard_map/deliver/pallas_call | solution.py:194
  (25 shorter events, 0.3 us)
Async XLA Ops:
  0.0 8.3 %copy-start.6 = (bf16[32,96,5]{1,0,2:T(8,128)(2,1)S(1)}, bf16[32,96,5]{1,0,2:T(8,128)(2,1)}, u32[]{:S(2)}) copy-start(bf16[32,96,5]{1,0,2:T(8,128)(2,1)} %param.6) | copy-start | bytes 92164
  0.0 7.8 %collective-permute-start.2 = (bf16[5,32,96]{2,1,0:T(8,128)(2,1)}, bf16[5,32,96]{2,1,0:T(8,128)(2,1)S(1)}, u32[]{:S(2)}, u32[]{:S(2)}) collective-permute-start(bf16[5,32,96]{2,1,0:T(8,128)(2,1)} %bitcast.9), channel_id=1, source_target_pairs={{0,3},{1,0},{2,1},{3,2},{4,7},{5,4},{6,5},{7,6},{8,11},{9,8},{10,9... | collective-permute-start | bytes 92168 | tf_op jit(solution)/shard_map/ppermute | solution.py:139
  3.3 4.6 %collective-permute-start.1 = (bf16[5,32,96]{2,1,0:T(8,128)(2,1)}, bf16[5,32,96]{2,1,0:T(8,128)(2,1)S(1)}, u32[]{:S(2)}, u32[]{:S(2)}) collective-permute-start(bf16[5,32,96]{2,1,0:T(8,128)(2,1)} %bitcast.10), channel_id=1, source_target_pairs={{0,2},{1,3},{2,0},{3,1},{4,6},{5,7},{6,4},{7,5},{8,10},{9,11},{10,... | collective-permute-start | bytes 92168 | tf_op jit(solution)/shard_map/ppermute | solution.py:139
  3.8 4.5 %collective-permute-start = (bf16[5,32,96]{2,1,0:T(8,128)(2,1)}, bf16[5,32,96]{2,1,0:T(8,128)(2,1)S(1)}, u32[]{:S(2)}, u32[]{:S(2)}) collective-permute-start(bf16[5,32,96]{2,1,0:T(8,128)(2,1)} %bitcast.11), channel_id=1, source_target_pairs={{0,1},{1,2},{2,3},{3,0},{4,5},{5,6},{6,7},{7,4},{8,9},{9,10},{10,1... | collective-permute-start | bytes 92168 | tf_op jit(solution)/shard_map/ppermute | solution.py:139
  4.4 24.7 %collective-permute-start.3 = (bf16[11,6,48,96]{3,2,1,0:T(8,128)(2,1)}, bf16[11,6,48,96]{3,2,1,0:T(8,128)(2,1)S(1)}, u32[]{:S(2)}, u32[]{:S(2)}) collective-permute-start(bf16[11,6,48,96]{3,2,1,0:T(8,128)(2,1)} %bitcast.7), channel_id=1, source_target_pairs={{0,4},{4,0},{1,5},{5,1},{2,6},{6,2},{3,7},{7,3},{8,12},{12,8},{9,1... | collective-permute-start | bytes 1824776 | tf_op jit(solution)/shard_map/ppermute | solution.py:135
  7.8 13.3 %copy-start.7 = (s32[11,1280]{1,0:T(8,128)S(1)}, s32[11,1280]{1,0:T(8,128)}, u32[]{:S(2)}) copy-start(s32[11,1280]{1,0:T(8,128)} %param.9) | copy-start | bytes 168964
  7.8 13.3 %copy-start.8 = (s32[11,1280]{1,0:T(8,128)S(1)}, s32[11,1280]{1,0:T(8,128)}, u32[]{:S(2)}) copy-start(s32[11,1280]{1,0:T(8,128)} %param.10) | copy-start | bytes 168964
  7.8 13.4 %copy-start.5 = (f32[11,1280]{1,0:T(8,128)S(1)}, f32[11,1280]{1,0:T(8,128)}, u32[]{:S(2)}) copy-start(f32[11,1280]{1,0:T(8,128)} %refs_2_.1) | copy-start | bytes 168964
  9.5 23.2 %all-to-all-start = ((bf16[32,32,128]{2,1,0:T(8,128)(2,1)}), bf16[32,32,128]{2,1,0:T(8,128)(2,1)}, u32[]{:S(2)}, u32[]{:S(2)}) async-start(bf16[32,32,128]{2,1,0:T(8,128)(2,1)} %bitcast.1), calls=%async_computation | async-start | bytes 524288 | tf_op jit(solution)/shard_map/all_to_all | solution.py:149
  28.1 1.0 %copy-start = (bf16[320,1792]{1,0:T(8,128)(2,1)}, bf16[320,1792]{1,0:T(8,128)(2,1)S(1)}, u32[]{:S(2)}) copy-start(bf16[320,1792]{1,0:T(8,128)(2,1)S(1)} %get-tuple-element.10.refs_3_) | copy-start | bytes 3440644
  29.1 0.9 %copy-start.3 = (bf16[11,6,48,96]{3,2,1,0:T(8,128)(2,1)}, bf16[11,6,48,96]{3,2,1,0:T(8,128)(2,1)S(1)}, u32[]{:S(2)}) copy-start(bf16[11,6,48,96]{3,2,1,0:T(8,128)(2,1)S(1)} %collective-permute-done.3.theirs_ref) | copy-start | bytes 1824772
  30.0 1.1 %copy-start.2 = (bf16[11,48,6,96]{3,1,2,0:T(8,128)(2,1)S(1)}, bf16[11,48,6,96]{3,1,2,0:T(8,128)(2,1)}, u32[]{:S(2)}) copy-start(bf16[11,48,6,96]{3,1,2,0:T(8,128)(2,1)} %param.7) | copy-start | bytes 1824772
  31.2 1.1 %copy-start.4 = (bf16[11,6,48,96]{3,2,1,0:T(8,128)(2,1)S(1)}, bf16[11,6,48,96]{3,2,1,0:T(8,128)(2,1)}, u32[]{:S(2)}) copy-start(bf16[11,6,48,96]{3,2,1,0:T(8,128)(2,1)} %copy-done.3) | copy-start | bytes 1824772
  32.7 1.3 %copy-start.1 = (bf16[320,1792]{1,0:T(8,128)(2,1)S(1)}, bf16[320,1792]{1,0:T(8,128)(2,1)}, u32[]{:S(2)}) copy-start(bf16[320,1792]{1,0:T(8,128)(2,1)} %copy-done) | copy-start | bytes 3440644
  36.8 3.5 %collective-permute-start.4 = (f32[160,128]{1,0:T(8,128)S(1)}, f32[160,128]{1,0:T(8,128)S(1)}, u32[]{:S(2)}, u32[]{:S(2)}) collective-permute-start(f32[160,128]{1,0:T(8,128)S(1)} %get-tuple-element.12), channel_id=1, source_target_pairs={{0,4},{4,0},{1,5},{5,1},{2,6},{6,2},{3,7},{7,3},{8,12},{12,8},{9,1... | collective-permute-start | bytes 245768 | tf_op jit(solution)/shard_map/ppermute | solution.py:186

commit v2 on v1

v2 whole, which is shorter than its diff:
```python
import math

import jax
import jax.numpy as jnp
from jax import lax
from jax.experimental import pallas as pl
from jax.experimental.pallas import tpu as pltpu
from jax.sharding import Mesh, PartitionSpec as P


LANES = 128
BF16 = jnp.bfloat16
F32 = jnp.float32


def split_two(value):
    high = value.astype(BF16)
    return high, (value - high.astype(F32)).astype(BF16)


def call(body, outs, scratch=(), vmem=12, **specs):
    return pl.pallas_call(
        body,
        out_shape=outs,
        scratch_shapes=scratch,
        compiler_params=pltpu.CompilerParams(vmem_limit_bytes=vmem << 20),
        **specs,
    )


def in_hbm(array):
    return pltpu.with_memory_space_constraint(array, pltpu.HBM)


NT = (((1,), (1,)), ((), ()))


def sublane_iota(count, width):
    return lax.broadcasted_iota(jnp.int32, (count, width), 0).astype(F32).astype(BF16)


def spans(modes, half):
    step = LANES // math.gcd(LANES, half)
    starts = range(0, modes, step)
    return [(k, min(k + step, modes), -(-(min(k + step, modes) - k) * half // LANES) * LANES) for k in starts]


def prepare_kernel(half, groups, where_ref, near_ref, far_ref, cols_ref, high_ref, low_ref, mine_hbm, theirs, *refs):
    count = len(groups)
    couplings, rows_out = refs[:count], refs[count]
    totals, splits = refs[count + 1 : 2 * count + 1], refs[2 * count + 1 : 3 * count + 1]
    every_row, weights, mine, in_sem, out_sem = refs[3 * count + 1 :]
    modes, slots, rows, block = mine.shape
    pairs = cols_ref.shape[1]
    load = pltpu.make_async_copy(mine_hbm, mine, in_sem)
    load.start()
    one, zero = jnp.ones((), BF16), jnp.zeros((), BF16)
    iota = sublane_iota(half, pairs)
    stores = []
    for group, (first, last, _) in enumerate(groups):
        total = totals[group]
        if last == modes:
            total[...] = jnp.zeros_like(total)
        for mode in range(first, last):
            at, slot = slice(mode, mode + 1), mode % 2
            hit = iota == cols_ref[at, :]
            weights[slot, :half, :] = jnp.where(hit, high_ref[at, :], zero)
            weights[slot, half:, :] = jnp.where(hit, low_ref[at, :], zero)
            for side, ref in enumerate((near_ref, far_ref)):
                every_row[slot, side * half : (side + 1) * half, :] = jnp.where(iota == ref[at, :], one, zero)
            got = lax.dot_general(every_row[slot], weights[slot, :half], NT, preferred_element_type=F32)
            got += lax.dot_general(every_row[slot], weights[slot, half:], NT, preferred_element_type=F32)
            total[:, (mode - first) * half : (mode - first + 1) * half] = got
        splits[group][0], splits[group][1] = split_two(total[...])
        store = pltpu.make_async_copy(splits[group], couplings[group], out_sem.at[group])
        store.start()
        stores.append(store)
        if group == 0:
            core = where_ref[1]
            rows_out[...] = jnp.zeros_like(rows_out)
            load.wait()
            for ref, part in ((mine, core), (theirs, 1 - core)):
                start = pl.multiple_of(part * rows, 16)
                for mode in range(modes):
                    for slot in range(slots):
                        lanes = slice(slot * LANES, slot * LANES + block)
                        rows_out[mode, pl.ds(start, rows), lanes] = ref[mode, slot]
    for store in stores:
        store.wait()


def tables_kernel(own, where_ref, *refs):
    (held_hbm, *tables_hbm), (held_ref, out_ref, near_ref, far_ref, at_ref, high_ref, low_ref) = refs[:5], refs[5:12]
    columns_ref, rows_ref, cols_ref, vals_ref, table, sem = refs[12:]
    targets = (columns_ref, rows_ref, cols_ref, vals_ref, held_ref)
    loads = [
        pltpu.make_async_copy(hbm, target, sem.at[at])
        for at, (hbm, target) in enumerate(zip((*tables_hbm, held_hbm), targets))
    ]
    for load in loads:
        load.start()
    for load in loads:
        load.wait()
    me, core = where_ref[0], where_ref[1]
    slots, nodes = columns_ref.shape
    columns = columns_ref[...]
    bits = nodes.bit_length() - 1
    away = jnp.bitwise_and(me - jnp.right_shift(columns, bits), LANES // nodes - 1)
    place = away * nodes + jnp.bitwise_and(columns, nodes - 1)
    table[...] = jnp.zeros_like(table)
    table[:slots, :nodes] = place.astype(F32)
    upright = table[...].T
    lanes = lax.broadcasted_iota(jnp.int32, (nodes, LANES), 1).astype(F32)
    for slot in range(slots):
        hit = upright[:nodes, slot : slot + 1] == lanes
        out_ref[slot * nodes : (slot + 1) * nodes, :] = jnp.where(hit, 1.0, 0.0).astype(BF16)

    def share(index):
        part = jnp.right_shift(index * (65536 // (2 * own) + 1), 16)
        rest = index - part * (2 * own)
        other = jnp.where(rest >= own, 1, 0)
        return (part * own + rest - other * own).astype(F32), other == core

    row_at, row_mine = share(rows_ref[...])
    col_at, col_mine = share(cols_ref[...])
    near_ref[...] = jnp.where(row_mine, row_at, -1.0).astype(BF16)
    far_ref[...] = jnp.where(row_mine, -1.0, row_at).astype(BF16)
    at_ref[...] = jnp.where(col_mine, col_at, -1.0).astype(BF16)
    high_ref[...], low_ref[...] = split_two(vals_ref[...])


def send_kernel(unit, select_ref, a_ref, b_ref, c_ref, d_ref, out_ref, held, wide):
    own, nodes, block = a_ref.shape
    slots = select_ref.shape[0] // nodes
    held[...] = jnp.zeros_like(held)
    for ref_at, ref in enumerate((a_ref, b_ref, c_ref, d_ref)):
        for i in range(own):
            held[i, ref_at * nodes : (ref_at + 1) * nodes, :block] = ref[i]
    select = select_ref[...]
    for i in range(own):
        got = jnp.dot(select, held[i], preferred_element_type=F32)
        for slot in range(slots):
            wide[pl.ds(own * slot + i, nodes, stride=unit), :] = got[slot * nodes : (slot + 1) * nodes]
    for line in range(own * slots, unit):
        wide[pl.ds(line, nodes, stride=unit), :] = jnp.zeros((nodes, LANES), F32)
    out_ref[...] = wide[...].astype(BF16)


def apply_kernel(own, slots, groups, got_ref, rows_ref, *refs):
    count = len(groups)
    couplings, (mine_ref, theirs_ref, wide, slotted), refs = refs[:count], refs[count : count + 4], refs[count + 4 :]
    splits, stacks, sem = refs[:count], refs[count : 2 * count], refs[2 * count]
    loads = [pltpu.make_async_copy(couplings[at], splits[at], sem.at[at]) for at in range(count)]
    for load in loads:
        load.start()
    parts, unit, _ = got_ref.shape
    half = own * parts
    wide[: parts * unit, :] = got_ref[...].reshape(parts * unit, LANES).astype(F32)
    wide[parts * unit :, :] = jnp.zeros((8, LANES), F32)
    for slot in range(slots):
        for part in range(parts):
            slotted[slot, pl.ds(own * part, 8), :] = wide[pl.ds(unit * part + own * slot, 8), :]
    held = jnp.concatenate([slotted[slot, :half, :].astype(BF16) for slot in range(slots)], axis=1)
    total = jnp.zeros((2 * half, LANES), F32)
    for at, (first, last, width) in enumerate(groups):
        lines = (last - first) * LANES
        some_rows = rows_ref[first:last].reshape(lines, slots * LANES)
        products = lax.dot_general(held, some_rows, NT, preferred_element_type=F32)
        stack = stacks[at]
        if (last - first) * half < width:
            stack[(last - first) * half :, :] = jnp.zeros_like(stack[(last - first) * half :, :])
        for mode in range(last - first):
            high, low = split_two(products[:, mode * LANES : (mode + 1) * LANES])
            stack[mode * half : (mode + 1) * half, :LANES] = high
            stack[mode * half : (mode + 1) * half, LANES:] = low
    for at in range(count):
        loads[at].wait()
        both = jnp.dot(splits[at][0], stacks[at][...], preferred_element_type=F32)
        total += both[:, :LANES] + both[:, LANES:]
        total += jnp.dot(splits[at][1], stacks[at][:, :LANES], preferred_element_type=F32)
    mine_ref[...] = total[:half]
    theirs_ref[...] = total[half:]


def finish_kernel(own, mine_ref, other_ref, out_ref, total):
    parts = out_ref.shape[0]
    half = own * parts
    total[:half, :] = mine_ref[...] + other_ref[...]
    total[half:, :] = jnp.zeros((8, LANES), F32)
    for part in range(parts):
        out_ref[part] = total[pl.ds(own * part, 8), :].astype(BF16)


def deliver_kernel(got_ref, out_ref, wide):
    own, nodes, block = out_ref.shape
    wide[...] = got_ref[...].reshape(nodes * 8, LANES).astype(F32)
    for i in range(own):
        out_ref[i] = wide[pl.ds(i, nodes, stride=8), :][:, :block].astype(BF16)


def compute(coefficients, stiffness, columns, pair_rows, pair_cols, pair_vals):
    nodes, block, own = coefficients.shape
    modes, _, slots, _ = stiffness.shape
    pairs = pair_rows.shape[1]
    parts = lax.axis_size("chip")
    meshes = lax.axis_size("mesh")
    half = own * parts
    unit = 32
    where = jnp.stack([lax.axis_index("mesh"), lax.axis_index("core")]).astype(jnp.int32)

    swap = [(0, 1), (1, 0)]
    held = jnp.transpose(coefficients, (2, 0, 1))
    around = {}
    for d in (2, 1, 3):
        around[d] = lax.ppermute(held, "mesh", [(i, (i + d) % meshes) for i in range(meshes)])
    smem = pl.BlockSpec(memory_space=pltpu.SMEM)
    vmem = pl.BlockSpec(memory_space=pltpu.VMEM)
    hbm = pl.BlockSpec(memory_space=pltpu.HBM)
    entries = jax.ShapeDtypeStruct((modes, pairs), BF16)
    held, select, *tables = call(
        lambda *refs: tables_kernel(own, *refs),
        [jax.ShapeDtypeStruct(held.shape, BF16), jax.ShapeDtypeStruct((slots * nodes, LANES), BF16)] + [entries] * 5,
        [pltpu.VMEM((slots, nodes), jnp.int32)]
        + [pltpu.VMEM((modes, pairs), x.dtype) for x in (pair_rows, pair_cols, pair_vals)]
        + [pltpu.VMEM((8, LANES), F32), pltpu.SemaphoreType.DMA((5,))],
        in_specs=[smem] + [hbm] * 5,
    )(where, *map(in_hbm, (held, columns.T, pair_rows, pair_cols, pair_vals)))
    mine = jnp.transpose(stiffness, (0, 2, 1, 3))
    mine, select = lax.optimization_barrier((mine, select))
    theirs = lax.ppermute(mine, "core", swap)
    outgoing = call(
        lambda *refs: send_kernel(unit, *refs),
        jax.ShapeDtypeStruct((parts * unit, LANES), BF16),
        [pltpu.VMEM((own, LANES, LANES), BF16), pltpu.VMEM((parts * unit, LANES), F32)],
    )(select, held, *(around[d] for d in (1, 2, 3)))
    got = lax.all_to_all(outgoing.reshape(parts, unit, LANES), "chip", 0, 0, tiled=True)

    groups = spans(modes, half)
    pieces = [(2, 2 * half, width) for _, _, width in groups]
    *couplings, all_rows = call(
        lambda *refs: prepare_kernel(half, groups, *refs),
        [pltpu.HBM(piece, BF16) for piece in pieces]
        + [jax.ShapeDtypeStruct((modes, LANES, slots * LANES), BF16)],
        [pltpu.VMEM(piece[1:], F32) for piece in pieces]
        + [pltpu.VMEM(piece, BF16) for piece in pieces]
        + [pltpu.VMEM((2, 2 * half, pairs), BF16)] * 2
        + [pltpu.VMEM(mine.shape, BF16)]
        + [pltpu.SemaphoreType.DMA, pltpu.SemaphoreType.DMA((len(groups),))],
        in_specs=[smem] + [vmem] * 5 + [hbm, vmem],
        out_specs=[hbm] * len(groups) + [vmem],
        vmem=32,
    )(where, *tables, in_hbm(mine), theirs)

    partial, other = call(
        lambda *refs: apply_kernel(own, slots, groups, *refs),
        [jax.ShapeDtypeStruct((half, LANES), F32)] * 2,
        [pltpu.VMEM((parts * unit + 8, LANES), F32), pltpu.VMEM((slots, half + 8, LANES), F32)]
        + [pltpu.VMEM(piece, BF16) for piece in pieces]
        + [pltpu.VMEM((piece[2], 2 * LANES), BF16) for piece in pieces]
        + [pltpu.SemaphoreType.DMA((len(groups),))],
        in_specs=[vmem] * 2 + [hbm] * len(groups),
        out_specs=[vmem] * 2,
        vmem=32,
    )(got, all_rows, *map(in_hbm, couplings))
    other = lax.ppermute(other, "core", swap)
    finished = call(
        lambda *refs: finish_kernel(own, *refs),
        jax.ShapeDtypeStruct((parts, 8, LANES), BF16),
        [pltpu.VMEM((half + 8, LANES), F32)],
    )(partial, other)
    returned = lax.all_to_all(finished, "chip", 0, 0, tiled=True)
    out = call(
        deliver_kernel, jax.ShapeDtypeStruct((own, nodes, block), BF16), [pltpu.VMEM((nodes * 8, LANES), F32)]
    )(returned)
    return jnp.transpose(out, (1, 2, 0))


def solution(mesh):
    chaos, meshes = mesh.devices.shape
    chips = Mesh(mesh.devices.reshape(chaos // 2, 2, meshes), ("chip", "core", "mesh"))
    spread = ("chip", "core")
    return jax.shard_map(
        compute,
        mesh=chips,
        in_specs=(
            P("mesh", None, spread),
            P(None, ("mesh", *spread), None, None),
            P("mesh", None),
            P(),
            P(),
            P(),
        ),
        out_specs=P("mesh", None, spread),
        check_vma=False,
    )
```

time: 59.2 us -> 56.2 us (0.949)
  local copies, waits for them, and re-layouts: 6.19 us -> 0 us
  waiting for transfers between devices: 1.42 us -> 5.65 us
  blocking collectives: 17.9 us -> 14 us
  Pallas kernels: 12.2 us -> 15 us
  starting transfers between devices: 20 us -> 21.1 us
  other arithmetic: 0.95 us -> 0.07 us
    unnamed x19 -> x0, local copies, waits for them, and re-layouts: 5.55 us -> none
    all_to_all x1, blocking collectives: 17.9 us -> 14 us  [compute(): returned = lax.all_to_all(finished, 'chip', 0, 0, tiled=True)]
    pallas_call x7 -> x6, Pallas kernels: 12.2 us -> 15 us  [the longest x1 8.18 us: compute(): call(lambda *refs: prepare_kernel(half, groups, *refs), [pltpu.HBM(piece,...]
    all_to_all x1, waiting for transfers between devices: 0.01 us -> 2.21 us  [compute(): lax.all_to_all(outgoing.reshape(parts, unit, LANES), 'chip', 0, 0, tiled=...]
    ppermute x5, waiting for transfers between devices: 1.42 us -> 3.45 us  [the longest x3 2.52 us: compute(): lax.ppermute(held, 'mesh', [(i, (i + d) % meshes) for i in range(meshes)])]
    ppermute x5, starting transfers between devices: 8.47 us -> 10.2 us  [the longest x1 3.84 us: compute(): other = lax.ppermute(other, 'core', swap)]
    add x3 -> x0, other arithmetic: 0.95 us -> none  [the longest x1 0.71 us: local(): lax.rem(me - columns // nodes + meshes, meshes) * (own * nodes)]
    all_to_all x1, starting transfers between devices: 11.5 us -> 10.8 us  [compute(): lax.all_to_all(outgoing.reshape(parts, unit, LANES), 'chip', 0, 0, tiled=...]
  transfers between devices with their start and end apart: 6 -> 6, of which waited for: 3 -> 4; matrix products, arithmetic and copies ran while one was open for 3% -> 0% of each run, Pallas kernels for 13% -> 17%
where the time goes in v2:
time: 56.2 us; the launch traced here: 55.8 us
  starting transfers between devices  21.1 us (38%)
  Pallas kernels  15 us (27%)
  blocking collectives  14 us (25%)
  waiting for transfers between devices  5.65 us (10%)
    all_to_all x1, blocking collectives, compute(): returned = lax.all_to_all(finished, 'chip', 0, 0, tiled=True)  14 us
    all_to_all x1, starting transfers between devices, compute(): lax.all_to_all(outgoing.reshape(parts, unit, LANES), 'chip', 0, 0, tiled=...  10.8 us
    pallas_call x1, Pallas kernels, compute(): call(lambda *refs: prepare_kernel(half, groups, *refs), [pltpu.HBM(piece,...  8.18 us
    ppermute x1, starting transfers between devices, compute(): other = lax.ppermute(other, 'core', swap)  3.84 us
    ppermute x1, starting transfers between devices, compute(): theirs = lax.ppermute(mine, 'core', swap)  3.29 us
    ppermute x3, starting transfers between devices, compute(): lax.ppermute(held, 'mesh', [(i, (i + d) % meshes) for i in range(meshes)])  3.11 us
    pallas_call x1, Pallas kernels, compute(): call(lambda *refs: apply_kernel(own, slots, groups, *refs), [jax.ShapeDty...  3.1 us
    ppermute x3, waiting for transfers between devices, compute(): lax.ppermute(held, 'mesh', [(i, (i + d) % meshes) for i in range(meshes)])  2.52 us
  transfers between devices with their start and end apart: 6, of which 4 were waited for; matrix products, arithmetic and copies ran while one was open for 0% of the time, Pallas kernels for 17%

profile of v2, /device:TPU:1, one launch (start us, length us, event | category | flops | bytes accessed | tf_op | source)
XLA Modules:
  0.0 55.8 jit_solution(9129300830348256203)
XLA Ops:
  0.0 0.1 pad_add_fusion.refs_0_
  0.1 1.8 %shard_map.64 = (bf16[5,32,96]{2,1,0:T(8,128)(2,1)S(1)}, bf16[192,128]{1,0:T(8,128)(2,1)S(1)}, bf16[11,1280]{1,0:T(8,128)(2,1)S(1)}, bf16[11,1280]{1,0:T(8,128)(...) custom-call(s32[2]{0:T(128)S(1)} %pad_add_fusion.refs_0_, ...), custom_call_target="tpu_custom_call" | custom-call | tf_op jit(solution)/shard_map/pallas_call | solution.py:220
  1.9 3.3 %collective-permute-start.3 = (bf16[11,6,48,96]{3,2,1,0:T(8,128)(2,1)}, bf16[11,6,48,96]{3,2,1,0:T(8,128)(2,1)S(1)}, u32[]{:S(2)}, u32[]{:S(2)}) collective-permute-start(bf16[11,6,48,96]{3,2,1,0:T(8,128)(2,1)} %bitcast.7), channel_id=1, source_target_pairs={{0,4},{4,0},{1,5},{5,1},{2,6},{6,2},{3,7},{7,3},{8,12},{12,8},{9,1... | collective-permute-start | bytes 1824776 | tf_op jit(solution)/shard_map/ppermute | solution.py:230
  5.2 0.0 collective-permute-start
  5.2 2.0 %collective-permute-start.1 = (bf16[5,32,96]{2,1,0:T(8,128)(2,1)}, bf16[5,32,96]{2,1,0:T(8,128)(2,1)S(1)}, u32[]{:S(2)}, u32[]{:S(2)}) collective-permute-start(bf16[5,32,96]{2,1,0:T(8,128)(2,1)} %bitcast.11), channel_id=1, source_target_pairs={{0,2},{1,3},{2,0},{3,1},{4,6},{5,7},{6,4},{7,5},{8,10},{9,11},{10,... | collective-permute-start | bytes 92168 | tf_op jit(solution)/shard_map/ppermute | solution.py:215
  7.1 1.2 %collective-permute-start.2 = (bf16[5,32,96]{2,1,0:T(8,128)(2,1)}, bf16[5,32,96]{2,1,0:T(8,128)(2,1)S(1)}, u32[]{:S(2)}, u32[]{:S(2)}) collective-permute-start(bf16[5,32,96]{2,1,0:T(8,128)(2,1)} %bitcast.12), channel_id=1, source_target_pairs={{0,3},{1,0},{2,1},{3,2},{4,7},{5,4},{6,5},{7,6},{8,11},{9,8},{10,9... | collective-permute-start | bytes 92168 | tf_op jit(solution)/shard_map/ppermute | solution.py:215
  8.3 1.9 %collective-permute-done.refs_2_ = bf16[5,32,96]{2,1,0:T(8,128)(2,1)S(1)} collective-permute-done((bf16[5,32,96]{2,1,0:T(8,128)(2,1)}, bf16[5,32,96]{2,1,0:T(8,128)(2,1)S(1)}, u32[]{:S(2)}, u32[]{:S(2)}) %collective-permute-start) | collective-permute-done | bytes 30752 | tf_op jit(solution)/shard_map/ppermute | solution.py:215
  10.2 0.0 collective-permute-done.1.refs_3_
  10.2 0.6 %collective-permute-done.2.refs_4_ = bf16[5,32,96]{2,1,0:T(8,128)(2,1)S(1)} collective-permute-done((bf16[5,32,96]{2,1,0:T(8,128)(2,1)}, bf16[5,32,96]{2,1,0:T(8,128)(2,1)S(1)}, u32[]{:S(2)}, u32[]{:S(2)}) %collective-permute-start.2) | collective-permute-done | bytes 30752 | tf_op jit(solution)/shard_map/ppermute | solution.py:215
  10.8 1.2 %shard_map.65 = bf16[1024,128]{1,0:T(8,128)(2,1)} custom-call(bf16[192,128]{1,0:T(8,128)(2,1)S(1)} %get-tuple-element.21.refs_0_, bf16[5,32,96]{2,1,0:T(8,128)(2,1)S(1)} %get-tuple-element.22.refs_1_, bf16[5,32,96]{2,1,0:T(8,128)(2,1)S(1)} %collective-permute-done.refs_2_, bf16[5,32,96]{2,1,0:T(8,128)(2,1)S(1)} %collective-permute-done.1.refs_3_, ...), custom_call_target="tpu_custom_call" | custom-call | tf_op jit(solution)/shard_map/pallas_call | solution.py:231
  12.0 10.8 %all-to-all-start = ((bf16[32,32,128]{2,1,0:T(8,128)(2,1)}), bf16[32,32,128]{2,1,0:T(8,128)(2,1)S(1)}, u32[]{:S(2)}, u32[]{:S(2)}) async-start(bf16[32,32,128]{2,1,0:T(8,128)(2,1)} %bitcast.5), calls=%async_computation | async-start | bytes 524288 | tf_op jit(solution)/shard_map/all_to_all | solution.py:236
  22.8 0.0 collective-permute-done.3.refs_7_
  22.9 8.2 %shard_map.66 = (bf16[2,320,640]{2,1,0:T(8,128)(2,1)}, bf16[2,320,640]{2,1,0:T(8,128)(2,1)}, bf16[2,320,512]{2,1,0:T(8,128)(2,1)}, bf16[11,128,768]{2,1,0:T(8,128)(2,1)S(1)}) custom-call(s32[2]{0:T(128)S(1)} %pad_add_fusion.refs_0_, bf16[11,1280]{1,0:T(8,128)(2,1)S(1)} %get-tuple-element.23.refs_1_, bf16[11,1280]{1,0:T(8,128)(2,1)S(1)} %get-tuple-element.24.refs_2_, ...), custom_call_target="tpu_custom_call" | custom-call | tf_op jit(solution)/shard_map/pallas_call | solution.py:240
  31.0 2.2 %all-to-all-done.refs_0_ = bf16[32,32,128]{2,1,0:T(8,128)(2,1)S(1)} async-done(((bf16[32,32,128]{2,1,0:T(8,128)(2,1)}), bf16[32,32,128]{2,1,0:T(8,128)(2,1)S(1)}, u32[]{:S(2)}, u32[]{:S(2)}) %all-to-all-start) | async-done | bytes 262176 | tf_op jit(solution)/shard_map/all_to_all | solution.py:236
  33.3 3.1 %shard_map.67 = (f32[160,128]{1,0:T(8,128)S(1)}, f32[160,128]{1,0:T(8,128)S(1)}) custom-call(bf16[32,32,128]{2,1,0:T(8,128)(2,1)S(1)} %all-to-all-done.refs_0_, bf16[11,128,768]{2,1,0:T(8,128)(2,1)S(1)} %get-tuple-element.29.refs_1_, bf16[2,320,640]{2,1,0:T(8,128)(2,1)} %get-tuple-element.30.refs_2_, bf16[2,320,640]{2,1,0:T(8,128)(2,1)} %get-tuple-element.31.refs_3_, ...), custom_call_target="tpu_custom_call" | custom-call | tf_op jit(solution)/shard_map/pallas_call | solution.py:254
  36.4 3.8 %collective-permute-start.4 = (f32[160,128]{1,0:T(8,128)S(1)}, f32[160,128]{1,0:T(8,128)S(1)}, u32[]{:S(2)}, u32[]{:S(2)}) collective-permute-start(f32[160,128]{1,0:T(8,128)S(1)} %get-tuple-element.34), channel_id=1, source_target_pairs={{0,4},{4,0},{1,5},{5,1},{2,6},{6,2},{3,7},{7,3},{8,12},{12,8},{9,1... | collective-permute-start | bytes 245768 | tf_op jit(solution)/shard_map/ppermute | solution.py:265
  40.2 0.9 %collective-permute-done.4.refs_1_ = f32[160,128]{1,0:T(8,128)S(1)} collective-permute-done((f32[160,128]{1,0:T(8,128)S(1)}, f32[160,128]{1,0:T(8,128)S(1)}, u32[]{:S(2)}, u32[]{:S(2)}) %collective-permute-start.4) | collective-permute-done | bytes 81952 | tf_op jit(solution)/shard_map/ppermute | solution.py:265
  41.2 14.0 %all_to_all.10.got_ref = bf16[32,8,128]{2,1,0:T(8,128)(2,1)S(1)} all-to-all(bf16[32,8,128]{2,1,0:T(8,128)(2,1)S(1)} %shard_map.68), channel_id=1, replica_groups=mesh['chip'=32,'core'=2,'mesh'=4] {'chip'}, dimensions={0} | all-to-all | bytes 131072 | tf_op jit(solution)/shard_map/all_to_all | solution.py:271
  55.2 0.6 %shard_map.69 = bf16[5,32,96]{2,1,0:T(8,128)(2,1)} custom-call(bf16[32,8,128]{2,1,0:T(8,128)(2,1)S(1)} %all_to_all.10.got_ref), custom_call_target="tpu_custom_call" | custom-call | tf_op jit(solution)/shard_map/pallas_call | solution.py:272
  (1 shorter events, 0.0 us)
Async XLA Ops:
  1.9 21.0 %collective-permute-start.3 = (bf16[11,6,48,96]{3,2,1,0:T(8,128)(2,1)}, bf16[11,6,48,96]{3,2,1,0:T(8,128)(2,1)S(1)}, u32[]{:S(2)}, u32[]{:S(2)}) collective-permute-start(bf16[11,6,48,96]{3,2,1,0:T(8,128)(2,1)} %bitcast.7), channel_id=1, source_target_pairs={{0,4},{4,0},{1,5},{5,1},{2,6},{6,2},{3,7},{7,3},{8,12},{12,8},{9,1... | collective-permute-start | bytes 1824776 | tf_op jit(solution)/shard_map/ppermute | solution.py:230
  5.2 5.0 %collective-permute-start = (bf16[5,32,96]{2,1,0:T(8,128)(2,1)}, bf16[5,32,96]{2,1,0:T(8,128)(2,1)S(1)}, u32[]{:S(2)}, u32[]{:S(2)}) collective-permute-start(bf16[5,32,96]{2,1,0:T(8,128)(2,1)} %bitcast.10), channel_id=1, source_target_pairs={{0,1},{1,2},{2,3},{3,0},{4,5},{5,6},{6,7},{7,4},{8,9},{9,10},{10,1... | collective-permute-start | bytes 92168 | tf_op jit(solution)/shard_map/ppermute | solution.py:215
  5.2 5.0 %collective-permute-start.1 = (bf16[5,32,96]{2,1,0:T(8,128)(2,1)}, bf16[5,32,96]{2,1,0:T(8,128)(2,1)S(1)}, u32[]{:S(2)}, u32[]{:S(2)}) collective-permute-start(bf16[5,32,96]{2,1,0:T(8,128)(2,1)} %bitcast.11), channel_id=1, source_target_pairs={{0,2},{1,3},{2,0},{3,1},{4,6},{5,7},{6,4},{7,5},{8,10},{9,11},{10,... | collective-permute-start | bytes 92168 | tf_op jit(solution)/shard_map/ppermute | solution.py:215
  7.1 3.7 %collective-permute-start.2 = (bf16[5,32,96]{2,1,0:T(8,128)(2,1)}, bf16[5,32,96]{2,1,0:T(8,128)(2,1)S(1)}, u32[]{:S(2)}, u32[]{:S(2)}) collective-permute-start(bf16[5,32,96]{2,1,0:T(8,128)(2,1)} %bitcast.12), channel_id=1, source_target_pairs={{0,3},{1,0},{2,1},{3,2},{4,7},{5,4},{6,5},{7,6},{8,11},{9,8},{10,9... | collective-permute-start | bytes 92168 | tf_op jit(solution)/shard_map/ppermute | solution.py:215
  12.0 21.2 %all-to-all-start = ((bf16[32,32,128]{2,1,0:T(8,128)(2,1)}), bf16[32,32,128]{2,1,0:T(8,128)(2,1)S(1)}, u32[]{:S(2)}, u32[]{:S(2)}) async-start(bf16[32,32,128]{2,1,0:T(8,128)(2,1)} %bitcast.5), calls=%async_computation | async-start | bytes 524288 | tf_op jit(solution)/shard_map/all_to_all | solution.py:236
  36.4 4.8 %collective-permute-start.4 = (f32[160,128]{1,0:T(8,128)S(1)}, f32[160,128]{1,0:T(8,128)S(1)}, u32[]{:S(2)}, u32[]{:S(2)}) collective-permute-start(f32[160,128]{1,0:T(8,128)S(1)} %get-tuple-element.34), channel_id=1, source_target_pairs={{0,4},{4,0},{1,5},{5,1},{2,6},{6,2},{3,7},{7,3},{8,12},{12,8},{9,1... | collective-permute-start | bytes 245768 | tf_op jit(solution)/shard_map/ppermute | solution.py:265

commit v3 on v2

v3 whole, which is shorter than its diff:
```python
import jax
import jax.numpy as jnp
from jax import lax
from jax.experimental import pallas as pl
from jax.experimental.pallas import tpu as pltpu
from jax.sharding import Mesh, PartitionSpec as P


LANES = 128
BF16 = jnp.bfloat16
F32 = jnp.float32


def split_two(value):
    high = value.astype(BF16)
    return high, (value - high.astype(F32)).astype(BF16)


def call(body, outs, scratch=(), vmem=12, **specs):
    return pl.pallas_call(
        body,
        out_shape=outs,
        scratch_shapes=scratch,
        compiler_params=pltpu.CompilerParams(vmem_limit_bytes=vmem << 20),
        **specs,
    )


def in_hbm(array):
    return pltpu.with_memory_space_constraint(array, pltpu.HBM)


TAIL = 3 * LANES
NT = (((1,), (1,)), ((), ()))


def sublane_iota(count, width):
    return lax.broadcasted_iota(jnp.int32, (count, width), 0).astype(F32).astype(BF16)


def prepare_kernel(half, near_ref, far_ref, cols_ref, high_ref, low_ref, out_ref, every_row, weights):
    modes, pairs = cols_ref.shape
    one, zero = jnp.ones((), BF16), jnp.zeros((), BF16)
    iota = sublane_iota(half, pairs)
    for mode in range(modes):
        at, slot = slice(mode, mode + 1), mode % 2
        hit = iota == cols_ref[at, :]
        weights[slot, :half, :] = jnp.where(hit, high_ref[at, :], zero)
        weights[slot, half:, :] = jnp.where(hit, low_ref[at, :], zero)
        for side, ref in enumerate((near_ref, far_ref)):
            every_row[slot, side * half : (side + 1) * half, :] = jnp.where(iota == ref[at, :], one, zero)
        got = lax.dot_general(weights[slot], every_row[slot], NT, preferred_element_type=F32)
        high, low = split_two(got[:half] + got[half:])
        lines = slice(mode * half, (mode + 1) * half)
        out_ref[lines, : 2 * half] = high
        out_ref[lines, 2 * half : TAIL] = low[:, 2 * LANES :]
        out_ref[lines, TAIL:] = low[:, : 2 * LANES]


def tables_kernel(own, where_ref, *refs):
    (held_hbm, *tables_hbm), (held_ref, out_ref, near_ref, far_ref, at_ref, high_ref, low_ref) = refs[:5], refs[5:12]
    columns_ref, rows_ref, cols_ref, vals_ref, table, sem = refs[12:]
    targets = (columns_ref, rows_ref, cols_ref, vals_ref, held_ref)
    loads = [
        pltpu.make_async_copy(hbm, target, sem.at[at])
        for at, (hbm, target) in enumerate(zip((*tables_hbm, held_hbm), targets))
    ]
    for load in loads:
        load.start()
    for load in loads:
        load.wait()
    me, core = where_ref[0], where_ref[1]
    slots, nodes = columns_ref.shape
    columns = columns_ref[...]
    bits = nodes.bit_length() - 1
    away = jnp.bitwise_and(me - jnp.right_shift(columns, bits), LANES // nodes - 1)
    place = away * nodes + jnp.bitwise_and(columns, nodes - 1)
    table[...] = jnp.zeros_like(table)
    table[:slots, :nodes] = place.astype(F32)
    upright = table[...].T
    lanes = lax.broadcasted_iota(jnp.int32, (nodes, LANES), 1).astype(F32)
    for slot in range(slots):
        hit = upright[:nodes, slot : slot + 1] == lanes
        out_ref[slot * nodes : (slot + 1) * nodes, :] = jnp.where(hit, 1.0, 0.0).astype(BF16)

    def share(index):
        part = jnp.right_shift(index * (65536 // (2 * own) + 1), 16)
        rest = index - part * (2 * own)
        other = jnp.where(rest >= own, 1, 0)
        return (part * own + rest - other * own).astype(F32), other == core

    row_at, row_mine = share(rows_ref[...])
    col_at, col_mine = share(cols_ref[...])
    near_ref[...] = jnp.where(row_mine, row_at, -1.0).astype(BF16)
    far_ref[...] = jnp.where(row_mine, -1.0, row_at).astype(BF16)
    at_ref[...] = jnp.where(col_mine, col_at, -1.0).astype(BF16)
    high_ref[...], low_ref[...] = split_two(vals_ref[...])


def send_kernel(unit, select_ref, a_ref, b_ref, c_ref, d_ref, out_ref, held, wide):
    own, nodes, block = a_ref.shape
    slots = select_ref.shape[0] // nodes
    held[...] = jnp.zeros_like(held)
    for ref_at, ref in enumerate((a_ref, b_ref, c_ref, d_ref)):
        for i in range(own):
            held[i, ref_at * nodes : (ref_at + 1) * nodes, :block] = ref[i]
    select = select_ref[...]
    for i in range(own):
        got = jnp.dot(select, held[i], preferred_element_type=F32)
        for slot in range(slots):
            wide[pl.ds(own * slot + i, nodes, stride=unit), :] = got[slot * nodes : (slot + 1) * nodes]
    for line in range(own * slots, unit):
        wide[pl.ds(line, nodes, stride=unit), :] = jnp.zeros((nodes, LANES), F32)
    out_ref[...] = wide[...].astype(BF16)


def apply_kernel(own, where_ref, got_ref, theirs_ref, coupling_ref, mine_hbm, near_ref, far_ref, mine, wide, slotted, stack, sem):
    load = pltpu.make_async_copy(mine_hbm, mine, sem)
    load.start()
    core = where_ref[1]
    parts, unit, _ = got_ref.shape
    modes, slots, rows, block = mine.shape
    half = own * parts
    wide[: parts * unit, :] = got_ref[...].reshape(parts * unit, LANES).astype(F32)
    wide[parts * unit :, :] = jnp.zeros((8, LANES), F32)
    for slot in range(slots):
        for part in range(parts):
            slotted[slot, pl.ds(own * part, 8), :] = wide[pl.ds(unit * part + own * slot, 8), :]
    held = [slotted[slot, :half, :block].astype(BF16) for slot in range(slots)]
    for ref, part in ((theirs_ref, 1 - core), (mine, core)):
        if ref is mine:
            load.wait()
        products = jnp.zeros((modes * rows, half), F32)
        for slot in range(slots):
            lines = ref[:, slot].reshape(modes * rows, block)
            products += lax.dot_general(lines, held[slot], NT, preferred_element_type=F32)
        start = pl.multiple_of(part * rows, 16)
        for mode in range(modes):
            high, low = split_two(products[mode * rows : (mode + 1) * rows])
            stack[mode, pl.ds(start, rows), :] = high
            stack[mode, pl.ds(2 * rows + start, rows), :] = low
    first = jnp.zeros((4 * rows, TAIL), F32)
    second = jnp.zeros((2 * rows, 2 * LANES), F32)
    for mode in range(modes):
        lines = slice(mode * half, (mode + 1) * half)
        first += jnp.dot(stack[mode], coupling_ref[lines, :TAIL], preferred_element_type=F32)
        second += jnp.dot(stack[mode, : 2 * rows], coupling_ref[lines, TAIL:], preferred_element_type=F32)
    both = first[: 2 * rows] + first[2 * rows :]
    tail = first[: 2 * rows, 2 * half :]
    total = jnp.concatenate([both[:, : 2 * LANES] + second, both[:, 2 * LANES : 2 * half] + tail], axis=1)
    edge = jnp.zeros((2 * rows, TAIL - 2 * half), F32)
    upright = jnp.concatenate([total, edge], axis=1).T
    near_ref[:, : 2 * rows] = upright[:half]
    far_ref[:, : 2 * rows] = upright[half : 2 * half]
    near_ref[:, 2 * rows :] = jnp.zeros((half, LANES - 2 * rows), F32)
    far_ref[:, 2 * rows :] = jnp.zeros((half, LANES - 2 * rows), F32)


def finish_kernel(own, mine_ref, other_ref, out_ref, total):
    parts = out_ref.shape[0]
    half = own * parts
    total[:half, :] = mine_ref[...] + other_ref[...]
    total[half:, :] = jnp.zeros((8, LANES), F32)
    for part in range(parts):
        out_ref[part] = total[pl.ds(own * part, 8), :].astype(BF16)


def deliver_kernel(got_ref, out_ref, wide):
    own, nodes, block = out_ref.shape
    wide[...] = got_ref[...].reshape(nodes * 8, LANES).astype(F32)
    for i in range(own):
        out_ref[i] = wide[pl.ds(i, nodes, stride=8), :][:, :block].astype(BF16)


def compute(coefficients, stiffness, columns, pair_rows, pair_cols, pair_vals):
    nodes, block, own = coefficients.shape
    modes, rows, slots, _ = stiffness.shape
    pairs = pair_rows.shape[1]
    parts = lax.axis_size("chip")
    meshes = lax.axis_size("mesh")
    half = own * parts
    unit = 32
    where = jnp.stack([lax.axis_index("mesh"), lax.axis_index("core")]).astype(jnp.int32)

    swap = [(0, 1), (1, 0)]
    held = jnp.transpose(coefficients, (2, 0, 1))
    around = {}
    for d in (2, 1, 3):
        around[d] = lax.ppermute(held, "mesh", [(i, (i + d) % meshes) for i in range(meshes)])
    smem = pl.BlockSpec(memory_space=pltpu.SMEM)
    vmem = pl.BlockSpec(memory_space=pltpu.VMEM)
    hbm = pl.BlockSpec(memory_space=pltpu.HBM)
    entries = jax.ShapeDtypeStruct((modes, pairs), BF16)
    held, select, *tables = call(
        lambda *refs: tables_kernel(own, *refs),
        [jax.ShapeDtypeStruct(held.shape, BF16), jax.ShapeDtypeStruct((slots * nodes, LANES), BF16)] + [entries] * 5,
        [pltpu.VMEM((slots, nodes), jnp.int32)]
        + [pltpu.VMEM((modes, pairs), x.dtype) for x in (pair_rows, pair_cols, pair_vals)]
        + [pltpu.VMEM((8, LANES), F32), pltpu.SemaphoreType.DMA((5,))],
        in_specs=[smem] + [hbm] * 5,
    )(where, *map(in_hbm, (held, columns.T, pair_rows, pair_cols, pair_vals)))
    outgoing = call(
        lambda *refs: send_kernel(unit, *refs),
        jax.ShapeDtypeStruct((parts * unit, LANES), BF16),
        [pltpu.VMEM((own, LANES, LANES), BF16), pltpu.VMEM((parts * unit, LANES), F32)],
    )(select, held, *(around[d] for d in (1, 2, 3)))
    got = lax.all_to_all(outgoing.reshape(parts, unit, LANES), "chip", 0, 0, tiled=True)

    mine = jnp.transpose(stiffness, (0, 2, 1, 3))
    theirs = lax.ppermute(mine, "core", swap)
    coupling = call(
        lambda *refs: prepare_kernel(half, *refs),
        jax.ShapeDtypeStruct((modes * half, TAIL + 2 * LANES), BF16),
        [pltpu.VMEM((2, 2 * half, pairs), BF16)] * 2,
    )(*tables)
    partial, other = call(
        lambda *refs: apply_kernel(own, *refs),
        [jax.ShapeDtypeStruct((half, LANES), F32)] * 2,
        [
            pltpu.VMEM(mine.shape, BF16),
            pltpu.VMEM((parts * unit + 8, LANES), F32),
            pltpu.VMEM((slots, half + 8, LANES), F32),
            pltpu.VMEM((modes, 4 * rows, half), BF16),
            pltpu.SemaphoreType.DMA,
        ],
        in_specs=[smem] + [vmem] * 3 + [hbm],
    )(where, got, theirs, coupling, in_hbm(mine))
    other = lax.ppermute(other, "core", swap)
    finished = call(
        lambda *refs: finish_kernel(own, *refs),
        jax.ShapeDtypeStruct((parts, 8, LANES), BF16),
        [pltpu.VMEM((half + 8, LANES), F32)],
    )(partial, other)
    returned = lax.all_to_all(finished, "chip", 0, 0, tiled=True)
    out = call(
        deliver_kernel, jax.ShapeDtypeStruct((own, nodes, block), BF16), [pltpu.VMEM((nodes * 8, LANES), F32)]
    )(returned)
    return jnp.transpose(out, (1, 2, 0))


def solution(mesh):
    chaos, meshes = mesh.devices.shape
    chips = Mesh(mesh.devices.reshape(chaos // 2, 2, meshes), ("chip", "core", "mesh"))
    spread = ("chip", "core")
    return jax.shard_map(
        compute,
        mesh=chips,
        in_specs=(
            P("mesh", None, spread),
            P(None, ("mesh", *spread), None, None),
            P("mesh", None),
            P(),
            P(),
            P(),
        ),
        out_specs=P("mesh", None, spread),
        check_vma=False,
    )
```

time: 56.2 us -> 54.1 us (0.963)
  Pallas kernels: 15 us -> 13.1 us
  blocking collectives: 14 us -> 12.4 us
  waiting for transfers between devices: 5.65 us -> 7.24 us
    all_to_all x1, waiting for transfers between devices: 2.21 us -> 6.3 us  [compute(): lax.all_to_all(outgoing.reshape(parts, unit, LANES), 'chip', 0, 0, tiled=...]
    ppermute x3, starting transfers between devices: 3.11 us -> 5.63 us  [compute(): lax.ppermute(held, 'mesh', [(i, (i + d) % meshes) for i in range(meshes)])]
    ppermute x3, waiting for transfers between devices: 2.52 us -> 0.01 us  [compute(): lax.ppermute(held, 'mesh', [(i, (i + d) % meshes) for i in range(meshes)])]
    pallas_call x2, Pallas kernels: 11.3 us -> 9.46 us  [the longest x1 4.88 us: compute(): call(lambda *refs: prepare_kernel(half, *refs), jax.ShapeDtypeStruct((mod...]
    ppermute x1, starting transfers between devices: 3.29 us -> 1.52 us  [compute(): theirs = lax.ppermute(mine, 'core', swap)]
    all_to_all x1, blocking collectives: 14 us -> 12.4 us  [compute(): returned = lax.all_to_all(finished, 'chip', 0, 0, tiled=True)]
    ppermute x1, starting transfers between devices: 3.84 us -> 2.54 us  [compute(): other = lax.ppermute(other, 'core', swap)]
  transfers between devices with their start and end apart: 6 -> 6, of which waited for: 4 -> 2; matrix products, arithmetic and copies ran while one was open for 0% -> 0% of each run, Pallas kernels for 17% -> 15%
where the time goes in v3:
time: 54.1 us; the launch traced here: 53.8 us
  starting transfers between devices  20.9 us (39%)
  Pallas kernels  13.1 us (24%)
  blocking collectives  12.4 us (23%)
  waiting for transfers between devices  7.24 us (13%)
    all_to_all x1, blocking collectives, compute(): returned = lax.all_to_all(finished, 'chip', 0, 0, tiled=True)  12.4 us
    all_to_all x1, starting transfers between devices, compute(): lax.all_to_all(outgoing.reshape(parts, unit, LANES), 'chip', 0, 0, tiled=...  11.2 us
    all_to_all x1, waiting for transfers between devices, compute(): lax.all_to_all(outgoing.reshape(parts, unit, LANES), 'chip', 0, 0, tiled=...  6.3 us
    ppermute x3, starting transfers between devices, compute(): lax.ppermute(held, 'mesh', [(i, (i + d) % meshes) for i in range(meshes)])  5.63 us
    pallas_call x1, Pallas kernels, compute(): call(lambda *refs: prepare_kernel(half, *refs), jax.ShapeDtypeStruct((mod...  4.88 us
    pallas_call x1, Pallas kernels, compute(): call(lambda *refs: apply_kernel(own, *refs), [jax.ShapeDtypeStruct((half,...  4.57 us
    ppermute x1, starting transfers between devices, compute(): other = lax.ppermute(other, 'core', swap)  2.54 us
    pallas_call x1, Pallas kernels, compute(): call(lambda *refs: tables_kernel(own, *refs), [jax.ShapeDtypeStruct(held....  1.79 us
  transfers between devices with their start and end apart: 6, of which 2 were waited for; matrix products, arithmetic and copies ran while one was open for 0% of the time, Pallas kernels for 15%

profile of v3, /device:TPU:1, one launch (start us, length us, event | category | flops | bytes accessed | tf_op | source)
XLA Modules:
  0.0 53.8 jit_solution(15372807098776297061)
XLA Ops:
  0.0 2.0 %collective-permute-start = (bf16[5,32,96]{2,1,0:T(8,128)(2,1)}, bf16[5,32,96]{2,1,0:T(8,128)(2,1)S(1)}, u32[]{:S(2)}, u32[]{:S(2)}) collective-permute-start(bf16[5,32,96]{2,1,0:T(8,128)(2,1)} %bitcast.9), channel_id=1, source_target_pairs={{0,1},{1,2},{2,3},{3,0},{4,5},{5,6},{6,7},{7,4},{8,9},{9,10},{10,1... | collective-permute-start | bytes 92168 | tf_op jit(solution)/shard_map/ppermute | solution.py:189
  2.0 2.5 %collective-permute-start.1 = (bf16[5,32,96]{2,1,0:T(8,128)(2,1)}, bf16[5,32,96]{2,1,0:T(8,128)(2,1)S(1)}, u32[]{:S(2)}, u32[]{:S(2)}) collective-permute-start(bf16[5,32,96]{2,1,0:T(8,128)(2,1)} %bitcast.10), channel_id=1, source_target_pairs={{0,2},{1,3},{2,0},{3,1},{4,6},{5,7},{6,4},{7,5},{8,10},{9,11},{10,... | collective-permute-start | bytes 92168 | tf_op jit(solution)/shard_map/ppermute | solution.py:189
  4.5 1.2 %collective-permute-start.2 = (bf16[5,32,96]{2,1,0:T(8,128)(2,1)}, bf16[5,32,96]{2,1,0:T(8,128)(2,1)S(1)}, u32[]{:S(2)}, u32[]{:S(2)}) collective-permute-start(bf16[5,32,96]{2,1,0:T(8,128)(2,1)} %bitcast.11), channel_id=1, source_target_pairs={{0,3},{1,0},{2,1},{3,2},{4,7},{5,4},{6,5},{7,6},{8,11},{9,8},{10,9... | collective-permute-start | bytes 92168 | tf_op jit(solution)/shard_map/ppermute | solution.py:189
  5.6 1.5 %collective-permute-start.3 = (bf16[11,6,48,96]{3,2,1,0:T(8,128)(2,1)}, bf16[11,6,48,96]{3,2,1,0:T(8,128)(2,1)S(1)}, u32[]{:S(2)}, u32[]{:S(2)}) collective-permute-start(bf16[11,6,48,96]{3,2,1,0:T(8,128)(2,1)} %bitcast.7), channel_id=1, source_target_pairs={{0,4},{4,0},{1,5},{5,1},{2,6},{6,2},{3,7},{7,3},{8,12},{12,8},{9,1... | collective-permute-start | bytes 1824776 | tf_op jit(solution)/shard_map/ppermute | solution.py:210
  7.2 0.1 pad_add_fusion.refs_0_
  7.2 1.8 %shard_map.64 = (bf16[5,32,96]{2,1,0:T(8,128)(2,1)S(1)}, bf16[192,128]{1,0:T(8,128)(2,1)S(1)}, bf16[11,1280]{1,0:T(8,128)(2,1)S(1)}, bf16[11,1280]{1,0:T(8,128)(...) custom-call(s32[2]{0:T(128)S(1)} %pad_add_fusion.refs_0_, ...), custom_call_target="tpu_custom_call" | custom-call | tf_op jit(solution)/shard_map/pallas_call | solution.py:194
  9.0 0.0 collective-permute-done.refs_2_
  9.0 0.0 collective-permute-done.1.refs_3_
  9.0 0.0 collective-permute-done.2.refs_4_
  9.1 1.2 %shard_map.65 = bf16[1024,128]{1,0:T(8,128)(2,1)} custom-call(bf16[192,128]{1,0:T(8,128)(2,1)S(1)} %get-tuple-element.14.refs_0_, bf16[5,32,96]{2,1,0:T(8,128)(2,1)S(1)} %get-tuple-element.15.refs_1_, bf16[5,32,96]{2,1,0:T(8,128)(2,1)S(1)} %collective-permute-done.refs_2_, bf16[5,32,96]{2,1,0:T(8,128)(2,1)S(1)} %collective-permute-done.1.refs_3_, ...), custom_call_target="tpu_custom_call" | custom-call | tf_op jit(solution)/shard_map/pallas_call | solution.py:202
  10.3 11.2 %all-to-all-start = ((bf16[32,32,128]{2,1,0:T(8,128)(2,1)}), bf16[32,32,128]{2,1,0:T(8,128)(2,1)S(1)}, u32[]{:S(2)}, u32[]{:S(2)}) async-start(bf16[32,32,128]{2,1,0:T(8,128)(2,1)} %bitcast.4), calls=%async_computation | async-start | bytes 524288 | tf_op jit(solution)/shard_map/all_to_all | solution.py:207
  21.5 4.9 %shard_map.66.refs_3_ = bf16[1760,640]{1,0:T(8,128)(2,1)S(1)} custom-call(bf16[11,1280]{1,0:T(8,128)(2,1)S(1)} %get-tuple-element.16.refs_0_, bf16[11,1280]{1,0:T(8,128)(2,1)S(1)} %get-tuple-element.17.refs_1_, bf16[11,1280]{1,0:T(8,128)(2,1)S(1)} %get-tuple-element.18.refs_2_, bf16[11,1280]{1,0:T(8,128)(2,1)S(1)} %get-tuple-element.19.refs_3_, ...), custom_call_target="tpu_custom_call" | custom-call | tf_op jit(solution)/shard_map/pallas_call | solution.py:211
  26.4 6.3 %all-to-all-done.refs_1_ = bf16[32,32,128]{2,1,0:T(8,128)(2,1)S(1)} async-done(((bf16[32,32,128]{2,1,0:T(8,128)(2,1)}), bf16[32,32,128]{2,1,0:T(8,128)(2,1)S(1)}, u32[]{:S(2)}, u32[]{:S(2)}) %all-to-all-start) | async-done | bytes 262176 | tf_op jit(solution)/shard_map/all_to_all | solution.py:207
  32.7 0.0 collective-permute-done.3.refs_2_
  32.7 4.6 %shard_map.67 = (f32[160,128]{1,0:T(8,128)S(1)}, f32[160,128]{1,0:T(8,128)S(1)}) custom-call(s32[2]{0:T(128)S(1)} %pad_add_fusion.refs_0_, bf16[32,32,128]{2,1,0:T(8,128)(2,1)S(1)} %all-to-all-done.refs_1_, bf16[11,6,48,96]{3,2,1,0:T(8,128)(2,1)S(1)} %collective-permute-done.3.refs_2_, bf16[1760,640]{1,0:T(8,128)(2,1)S(1)} %shard_map.66.refs_3_, ...), custom_call_target="tpu_custom_call" | custom-call | tf_op jit(solution)/shard_map/pallas_call | solution.py:216
  37.3 2.5 %collective-permute-start.4 = (f32[160,128]{1,0:T(8,128)S(1)}, f32[160,128]{1,0:T(8,128)S(1)}, u32[]{:S(2)}, u32[]{:S(2)}) collective-permute-start(f32[160,128]{1,0:T(8,128)S(1)} %get-tuple-element.22), channel_id=1, source_target_pairs={{0,4},{4,0},{1,5},{5,1},{2,6},{6,2},{3,7},{7,3},{8,12},{12,8},{9,1... | collective-permute-start | bytes 245768 | tf_op jit(solution)/shard_map/ppermute | solution.py:228
  39.8 0.9 %collective-permute-done.4.refs_1_ = f32[160,128]{1,0:T(8,128)S(1)} collective-permute-done((f32[160,128]{1,0:T(8,128)S(1)}, f32[160,128]{1,0:T(8,128)S(1)}, u32[]{:S(2)}, u32[]{:S(2)}) %collective-permute-start.4) | collective-permute-done | bytes 81952 | tf_op jit(solution)/shard_map/ppermute | solution.py:228
  40.7 12.4 %all_to_all.10.got_ref = bf16[32,8,128]{2,1,0:T(8,128)(2,1)S(1)} all-to-all(bf16[32,8,128]{2,1,0:T(8,128)(2,1)S(1)} %shard_map.68), channel_id=1, replica_groups=mesh['chip'=32,'core'=2,'mesh'=4] {'chip'}, dimensions={0} | all-to-all | bytes 131072 | tf_op jit(solution)/shard_map/all_to_all | solution.py:234
  53.2 0.6 %shard_map.69 = bf16[5,32,96]{2,1,0:T(8,128)(2,1)} custom-call(bf16[32,8,128]{2,1,0:T(8,128)(2,1)S(1)} %all_to_all.10.got_ref), custom_call_target="tpu_custom_call" | custom-call | tf_op jit(solution)/shard_map/pallas_call | solution.py:235
  (1 shorter events, 0.0 us)
Async XLA Ops:
  0.0 9.0 %collective-permute-start = (bf16[5,32,96]{2,1,0:T(8,128)(2,1)}, bf16[5,32,96]{2,1,0:T(8,128)(2,1)S(1)}, u32[]{:S(2)}, u32[]{:S(2)}) collective-permute-start(bf16[5,32,96]{2,1,0:T(8,128)(2,1)} %bitcast.9), channel_id=1, source_target_pairs={{0,1},{1,2},{2,3},{3,0},{4,5},{5,6},{6,7},{7,4},{8,9},{9,10},{10,1... | collective-permute-start | bytes 92168 | tf_op jit(solution)/shard_map/ppermute | solution.py:189
  2.0 7.0 %collective-permute-start.1 = (bf16[5,32,96]{2,1,0:T(8,128)(2,1)}, bf16[5,32,96]{2,1,0:T(8,128)(2,1)S(1)}, u32[]{:S(2)}, u32[]{:S(2)}) collective-permute-start(bf16[5,32,96]{2,1,0:T(8,128)(2,1)} %bitcast.10), channel_id=1, source_target_pairs={{0,2},{1,3},{2,0},{3,1},{4,6},{5,7},{6,4},{7,5},{8,10},{9,11},{10,... | collective-permute-start | bytes 92168 | tf_op jit(solution)/shard_map/ppermute | solution.py:189
  4.5 4.6 %collective-permute-start.2 = (bf16[5,32,96]{2,1,0:T(8,128)(2,1)}, bf16[5,32,96]{2,1,0:T(8,128)(2,1)S(1)}, u32[]{:S(2)}, u32[]{:S(2)}) collective-permute-start(bf16[5,32,96]{2,1,0:T(8,128)(2,1)} %bitcast.11), channel_id=1, source_target_pairs={{0,3},{1,0},{2,1},{3,2},{4,7},{5,4},{6,5},{7,6},{8,11},{9,8},{10,9... | collective-permute-start | bytes 92168 | tf_op jit(solution)/shard_map/ppermute | solution.py:189
  5.6 27.0 %collective-permute-start.3 = (bf16[11,6,48,96]{3,2,1,0:T(8,128)(2,1)}, bf16[11,6,48,96]{3,2,1,0:T(8,128)(2,1)S(1)}, u32[]{:S(2)}, u32[]{:S(2)}) collective-permute-start(bf16[11,6,48,96]{3,2,1,0:T(8,128)(2,1)} %bitcast.7), channel_id=1, source_target_pairs={{0,4},{4,0},{1,5},{5,1},{2,6},{6,2},{3,7},{7,3},{8,12},{12,8},{9,1... | collective-permute-start | bytes 1824776 | tf_op jit(solution)/shard_map/ppermute | solution.py:210
  10.3 22.4 %all-to-all-start = ((bf16[32,32,128]{2,1,0:T(8,128)(2,1)}), bf16[32,32,128]{2,1,0:T(8,128)(2,1)S(1)}, u32[]{:S(2)}, u32[]{:S(2)}) async-start(bf16[32,32,128]{2,1,0:T(8,128)(2,1)} %bitcast.4), calls=%async_computation | async-start | bytes 524288 | tf_op jit(solution)/shard_map/all_to_all | solution.py:207
  37.3 3.5 %collective-permute-start.4 = (f32[160,128]{1,0:T(8,128)S(1)}, f32[160,128]{1,0:T(8,128)S(1)}, u32[]{:S(2)}, u32[]{:S(2)}) collective-permute-start(f32[160,128]{1,0:T(8,128)S(1)} %get-tuple-element.22), channel_id=1, source_target_pairs={{0,4},{4,0},{1,5},{5,1},{2,6},{6,2},{3,7},{7,3},{8,12},{12,8},{9,1... | collective-permute-start | bytes 245768 | tf_op jit(solution)/shard_map/ppermute | solution.py:228

commit v4 on v3

--- a/solution.py
+++ b/solution.py
@@ -38,10 +38,11 @@
     return lax.broadcasted_iota(jnp.int32, (count, width), 0).astype(F32).astype(BF16)
 
 
-def prepare_kernel(half, near_ref, far_ref, cols_ref, high_ref, low_ref, out_ref, every_row, weights):
+def prepare_kernel(half, near_ref, far_ref, cols_ref, high_ref, low_ref, out_ref, rest_hbm, every_row, weights, rest, sem):
     modes, pairs = cols_ref.shape
     one, zero = jnp.ones((), BF16), jnp.zeros((), BF16)
     iota = sublane_iota(half, pairs)
+    stores = []
     for mode in range(modes):
         at, slot = slice(mode, mode + 1), mode % 2
         hit = iota == cols_ref[at, :]
@@ -53,8 +54,13 @@
         high, low = split_two(got[:half] + got[half:])
         lines = slice(mode * half, (mode + 1) * half)
         out_ref[lines, : 2 * half] = high
-        out_ref[lines, 2 * half : TAIL] = low[:, 2 * LANES :]
-        out_ref[lines, TAIL:] = low[:, : 2 * LANES]
+        out_ref[lines, 2 * half :] = low[:, 2 * LANES :]
+        rest[lines, :] = low[:, : 2 * LANES]
+        store = pltpu.make_async_copy(rest.at[lines], rest_hbm.at[lines], sem.at[mode])
+        store.start()
+        stores.append(store)
+    for store in stores:
+        store.wait()
 
 
 def tables_kernel(own, where_ref, *refs):
@@ -73,7 +79,7 @@
     slots, nodes = columns_ref.shape
     columns = columns_ref[...]
     bits = nodes.bit_length() - 1
-    away = jnp.bitwise_and(me - jnp.right_shift(columns, bits), LANES // nodes - 1)
+    away = jnp.bitwise_and((me - jnp.right_shift(columns, bits)) * (1 - 2 * core), LANES // nodes - 1)
     place = away * nodes + jnp.bitwise_and(columns, nodes - 1)
     table[...] = jnp.zeros_like(table)
     table[:slots, :nodes] = place.astype(F32)
@@ -114,12 +120,12 @@
     out_ref[...] = wide[...].astype(BF16)
 
 
-def apply_kernel(own, where_ref, got_ref, theirs_ref, coupling_ref, mine_hbm, near_ref, far_ref, mine, wide, slotted, stack, sem):
-    load = pltpu.make_async_copy(mine_hbm, mine, sem)
+def apply_kernel(own, where_ref, got_ref, theirs_ref, mine_ref, coupling_ref, rest_hbm, near_ref, far_ref, rest, wide, slotted, stack, sem):
+    load = pltpu.make_async_copy(rest_hbm, rest, sem)
     load.start()
     core = where_ref[1]
     parts, unit, _ = got_ref.shape
-    modes, slots, rows, block = mine.shape
+    modes, slots, rows, block = mine_ref.shape
     half = own * parts
     wide[: parts * unit, :] = got_ref[...].reshape(parts * unit, LANES).astype(F32)
     wide[parts * unit :, :] = jnp.zeros((8, LANES), F32)
@@ -127,9 +133,7 @@
         for part in range(parts):
             slotted[slot, pl.ds(own * part, 8), :] = wide[pl.ds(unit * part + own * slot, 8), :]
     held = [slotted[slot, :half, :block].astype(BF16) for slot in range(slots)]
-    for ref, part in ((theirs_ref, 1 - core), (mine, core)):
-        if ref is mine:
-            load.wait()
+    for ref, part in ((theirs_ref, 1 - core), (mine_ref, core)):
         products = jnp.zeros((modes * rows, half), F32)
         for slot in range(slots):
             lines = ref[:, slot].reshape(modes * rows, block)
@@ -143,8 +147,11 @@
     second = jnp.zeros((2 * rows, 2 * LANES), F32)
     for mode in range(modes):
         lines = slice(mode * half, (mode + 1) * half)
-        first += jnp.dot(stack[mode], coupling_ref[lines, :TAIL], preferred_element_type=F32)
-        second += jnp.dot(stack[mode, : 2 * rows], coupling_ref[lines, TAIL:], preferred_element_type=F32)
+        first += jnp.dot(stack[mode], coupling_ref[lines, :], preferred_element_type=F32)
+    load.wait()
+    for mode in range(modes):
+        lines = slice(mode * half, (mode + 1) * half)
+        second += jnp.dot(stack[mode, : 2 * rows], rest[lines, :], preferred_element_type=F32)
     both = first[: 2 * rows] + first[2 * rows :]
     tail = first[: 2 * rows, 2 * half :]
     total = jnp.concatenate([both[:, : 2 * LANES] + second, both[:, 2 * LANES : 2 * half] + tail], axis=1)
@@ -184,9 +191,14 @@
 
     swap = [(0, 1), (1, 0)]
     held = jnp.transpose(coefficients, (2, 0, 1))
-    around = {}
-    for d in (2, 1, 3):
-        around[d] = lax.ppermute(held, "mesh", [(i, (i + d) % meshes) for i in range(meshes)])
+
+    def turn(block, way):
+        ways = [(c * meshes + m, c * meshes + (m + (way if c == 0 else -way)) % meshes) for c in range(2) for m in range(meshes)]
+        return lax.ppermute(block, ("core", "mesh"), ways)
+
+    behind = turn(held, 1)
+    ahead = turn(held, -1)
+    across = turn(behind, 1)
     smem = pl.BlockSpec(memory_space=pltpu.SMEM)
     vmem = pl.BlockSpec(memory_space=pltpu.VMEM)
     hbm = pl.BlockSpec(memory_space=pltpu.HBM)
@@ -203,28 +215,33 @@
         lambda *refs: send_kernel(unit, *refs),
         jax.ShapeDtypeStruct((parts * unit, LANES), BF16),
         [pltpu.VMEM((own, LANES, LANES), BF16), pltpu.VMEM((parts * unit, LANES), F32)],
-    )(select, held, *(around[d] for d in (1, 2, 3)))
+    )(select, held, behind, across, ahead)
     got = lax.all_to_all(outgoing.reshape(parts, unit, LANES), "chip", 0, 0, tiled=True)
 
     mine = jnp.transpose(stiffness, (0, 2, 1, 3))
     theirs = lax.ppermute(mine, "core", swap)
-    coupling = call(
+    coupling, rest = call(
         lambda *refs: prepare_kernel(half, *refs),
-        jax.ShapeDtypeStruct((modes * half, TAIL + 2 * LANES), BF16),
-        [pltpu.VMEM((2, 2 * half, pairs), BF16)] * 2,
+        [jax.ShapeDtypeStruct((modes * half, TAIL), BF16), pltpu.HBM((modes * half, 2 * LANES), BF16)],
+        [
+            *[pltpu.VMEM((2, 2 * half, pairs), BF16)] * 2,
+            pltpu.VMEM((modes * half, 2 * LANES), BF16),
+            pltpu.SemaphoreType.DMA((modes,)),
+        ],
+        out_specs=[vmem, hbm],
     )(*tables)
     partial, other = call(
         lambda *refs: apply_kernel(own, *refs),
         [jax.ShapeDtypeStruct((half, LANES), F32)] * 2,
         [
-            pltpu.VMEM(mine.shape, BF16),
+            pltpu.VMEM((modes * half, 2 * LANES), BF16),
             pltpu.VMEM((parts * unit + 8, LANES), F32),
             pltpu.VMEM((slots, half + 8, LANES), F32),
             pltpu.VMEM((modes, 4 * rows, half), BF16),
             pltpu.SemaphoreType.DMA,
         ],
-        in_specs=[smem] + [vmem] * 3 + [hbm],
-    )(where, got, theirs, coupling, in_hbm(mine))
+        in_specs=[smem] + [vmem] * 4 + [hbm],
+    )(where, got, theirs, mine, coupling, in_hbm(rest))
     other = lax.ppermute(other, "core", swap)
     finished = call(
         lambda *refs: finish_kernel(own, *refs),

time: 54.1 us -> 54.5 us (level)
  starting transfers between devices: 20.9 us -> 22.9 us
  waiting for transfers between devices: 7.24 us -> 5.84 us
    ppermute x1, starting transfers between devices: 2.54 us -> 4.17 us  [compute(): other = lax.ppermute(other, 'core', swap)]
    ppermute x1, starting transfers between devices: 1.52 us -> 3.14 us  [compute(): theirs = lax.ppermute(mine, 'core', swap)]
    all_to_all x1, waiting for transfers between devices: 6.3 us -> 4.91 us  [compute(): lax.all_to_all(outgoing.reshape(parts, unit, LANES), 'chip', 0, 0, tiled=...]
    ppermute x3, starting transfers between devices: 5.63 us -> 4.43 us  [turn(): return lax.ppermute(block, ('core', 'mesh'), ways)]
    pallas_call x1, Pallas kernels: 4.88 us -> 5.52 us  [compute(): call(lambda *refs: prepare_kernel(half, *refs), [jax.ShapeDtypeStruct((mo...]
    pallas_call x1, Pallas kernels: 4.57 us -> 3.98 us  [compute(): call(lambda *refs: apply_kernel(own, *refs), [jax.ShapeDtypeStruct((half,...]
  transfers between devices with their start and end apart: 6 -> 6, of which waited for: 2 -> 2; matrix products, arithmetic and copies ran while one was open for 0% -> 0% of each run, Pallas kernels for 15% -> 16%
where the time goes in v4:
time: 54.5 us; the launch traced here: 54.2 us
  starting transfers between devices  22.9 us (42%)
  Pallas kernels  13.2 us (24%)
  blocking collectives  12.1 us (22%)
  waiting for transfers between devices  5.84 us (11%)
    all_to_all x1, blocking collectives, compute(): returned = lax.all_to_all(finished, 'chip', 0, 0, tiled=True)  12.1 us
    all_to_all x1, starting transfers between devices, compute(): lax.all_to_all(outgoing.reshape(parts, unit, LANES), 'chip', 0, 0, tiled=...  11.2 us
    pallas_call x1, Pallas kernels, compute(): call(lambda *refs: prepare_kernel(half, *refs), [jax.ShapeDtypeStruct((mo...  5.52 us
    all_to_all x1, waiting for transfers between devices, compute(): lax.all_to_all(outgoing.reshape(parts, unit, LANES), 'chip', 0, 0, tiled=...  4.91 us
    ppermute x3, starting transfers between devices, turn(): return lax.ppermute(block, ('core', 'mesh'), ways)  4.43 us
    ppermute x1, starting transfers between devices, compute(): other = lax.ppermute(other, 'core', swap)  4.17 us
    pallas_call x1, Pallas kernels, compute(): call(lambda *refs: apply_kernel(own, *refs), [jax.ShapeDtypeStruct((half,...  3.98 us
    ppermute x1, starting transfers between devices, compute(): theirs = lax.ppermute(mine, 'core', swap)  3.14 us
  transfers between devices with their start and end apart: 6, of which 2 were waited for; matrix products, arithmetic and copies ran while one was open for 0% of the time, Pallas kernels for 16%

profile of v4, /device:TPU:1, one launch (start us, length us, event | category | flops | bytes accessed | tf_op | source)
XLA Modules:
  0.0 54.2 jit_solution(12953837003388313626)
XLA Ops:
  0.0 0.0 copy-start
  0.0 3.3 %collective-permute-start = (bf16[5,32,96]{2,1,0:T(8,128)(2,1)}, bf16[5,32,96]{2,1,0:T(8,128)(2,1)S(1)}, u32[]{:S(2)}, u32[]{:S(2)}) collective-permute-start(bf16[5,32,96]{2,1,0:T(8,128)(2,1)} %bitcast.9), channel_id=1, source_target_pairs={{0,1},{1,2},{2,3},{3,0},{4,7},{5,4},{6,5},{7,6},{8,9},{9,10},{10,1... | collective-permute-start | bytes 92168 | tf_op jit(solution)/shard_map/ppermute | solution.py:197
  3.3 0.0 collective-permute-start.2
  3.3 3.1 %collective-permute-start.3 = (bf16[11,6,48,96]{3,2,1,0:T(8,128)(2,1)}, bf16[11,6,48,96]{3,2,1,0:T(8,128)(2,1)S(1)}, u32[]{:S(2)}, u32[]{:S(2)}) collective-permute-start(bf16[11,6,48,96]{3,2,1,0:T(8,128)(2,1)} %bitcast.7), channel_id=1, source_target_pairs={{0,4},{4,0},{1,5},{5,1},{2,6},{6,2},{3,7},{7,3},{8,12},{12,8},{9,1... | collective-permute-start | bytes 1824776 | tf_op jit(solution)/shard_map/ppermute | solution.py:222
  6.4 0.0 collective-permute-done.refs_2_
  6.4 1.1 %collective-permute-start.1 = (bf16[5,32,96]{2,1,0:T(8,128)(2,1)S(1)}, bf16[5,32,96]{2,1,0:T(8,128)(2,1)S(1)}, u32[]{:S(2)}, u32[]{:S(2)}) collective-permute-start(bf16[5,32,96]{2,1,0:T(8,128)(2,1)S(1)} %collective-permute-done.refs_2_), channel_id=1, source_target_pairs={{0,1},{1,2},{2,3},{3,0},{4,7},{5,4},{6,5},{7,6},{8,9},{9,10},{10,1... | collective-permute-start | bytes 92168 | tf_op jit(solution)/shard_map/ppermute | solution.py:197
  7.6 0.1 pad_add_fusion.refs_0_
  7.6 1.8 %shard_map.64 = (bf16[5,32,96]{2,1,0:T(8,128)(2,1)S(1)}, bf16[192,128]{1,0:T(8,128)(2,1)S(1)}, bf16[11,1280]{1,0:T(8,128)(2,1)S(1)}, bf16[11,1280]{1,0:T(8,128)(...) custom-call(s32[2]{0:T(128)S(1)} %pad_add_fusion.refs_0_, ...), custom_call_target="tpu_custom_call" | custom-call | tf_op jit(solution)/shard_map/pallas_call | solution.py:206
  9.5 0.0 collective-permute-done.2.refs_4_
  9.5 0.0 collective-permute-done.1.refs_3_
  9.5 1.2 %shard_map.65 = bf16[1024,128]{1,0:T(8,128)(2,1)} custom-call(bf16[192,128]{1,0:T(8,128)(2,1)S(1)} %get-tuple-element.16.refs_0_, bf16[5,32,96]{2,1,0:T(8,128)(2,1)S(1)} %get-tuple-element.17.refs_1_, bf16[5,32,96]{2,1,0:T(8,128)(2,1)S(1)} %collective-permute-done.refs_2_, bf16[5,32,96]{2,1,0:T(8,128)(2,1)S(1)} %collective-permute-done.1.refs_3_, ...), custom_call_target="tpu_custom_call" | custom-call | tf_op jit(solution)/shard_map/pallas_call | solution.py:214
  10.7 11.2 %all-to-all-start = ((bf16[32,32,128]{2,1,0:T(8,128)(2,1)}), bf16[32,32,128]{2,1,0:T(8,128)(2,1)S(1)}, u32[]{:S(2)}, u32[]{:S(2)}) async-start(bf16[32,32,128]{2,1,0:T(8,128)(2,1)} %bitcast.4), calls=%async_computation | async-start | bytes 524288 | tf_op jit(solution)/shard_map/all_to_all | solution.py:219
  21.9 5.5 %shard_map.66 = (bf16[1760,384]{1,0:T(8,128)(2,1)S(1)}, bf16[1760,256]{1,0:T(8,128)(2,1)}) custom-call(bf16[11,1280]{1,0:T(8,128)(2,1)S(1)} %get-tuple-element.18.refs_0_, bf16[11,1280]{1,0:T(8,128)(2,1)S(1)} %get-tuple-element.19.refs_1_, bf16[11,1280]{1,0:T(8,128)(2,1)S(1)} %get-tuple-element.20.refs_2_, bf16[11,1280]{1,0:T(8,128)(2,1)S(1)} %get-tuple-element.21.refs_3_, ...), custom_call_target="tpu_custom_call" | custom-call | tf_op jit(solution)/shard_map/pallas_call | solution.py:223
  27.5 4.9 %all-to-all-done.refs_1_ = bf16[32,32,128]{2,1,0:T(8,128)(2,1)S(1)} async-done(((bf16[32,32,128]{2,1,0:T(8,128)(2,1)}), bf16[32,32,128]{2,1,0:T(8,128)(2,1)S(1)}, u32[]{:S(2)}, u32[]{:S(2)}) %all-to-all-start) | async-done | bytes 262176 | tf_op jit(solution)/shard_map/all_to_all | solution.py:219
  32.4 0.0 collective-permute-done.3.refs_2_
  32.4 0.0 copy-done
  32.4 4.0 %shard_map.67 = (f32[160,128]{1,0:T(8,128)S(1)}, f32[160,128]{1,0:T(8,128)S(1)}) custom-call(s32[2]{0:T(128)S(1)} %pad_add_fusion.refs_0_, bf16[32,32,128]{2,1,0:T(8,128)(2,1)S(1)} %all-to-all-done.refs_1_, bf16[11,6,48,96]{3,2,1,0:T(8,128)(2,1)S(1)} %collective-permute-done.3.refs_2_, bf16[11,6,48,96]{3,2,1,0:T(8,128)(2,1)S(1)} %bitcast.8, ...), custom_call_target="tpu_custom_call" | custom-call | tf_op jit(solution)/shard_map/pallas_call | solution.py:233
  36.4 4.2 %collective-permute-start.4 = (f32[160,128]{1,0:T(8,128)S(1)}, f32[160,128]{1,0:T(8,128)S(1)}, u32[]{:S(2)}, u32[]{:S(2)}) collective-permute-start(f32[160,128]{1,0:T(8,128)S(1)} %get-tuple-element.26), channel_id=1, source_target_pairs={{0,4},{4,0},{1,5},{5,1},{2,6},{6,2},{3,7},{7,3},{8,12},{12,8},{9,1... | collective-permute-start | bytes 245768 | tf_op jit(solution)/shard_map/ppermute | solution.py:245
  40.5 0.9 %collective-permute-done.4.refs_1_ = f32[160,128]{1,0:T(8,128)S(1)} collective-permute-done((f32[160,128]{1,0:T(8,128)S(1)}, f32[160,128]{1,0:T(8,128)S(1)}, u32[]{:S(2)}, u32[]{:S(2)}) %collective-permute-start.4) | collective-permute-done | bytes 81952 | tf_op jit(solution)/shard_map/ppermute | solution.py:245
  41.5 12.1 %all_to_all.10.got_ref = bf16[32,8,128]{2,1,0:T(8,128)(2,1)S(1)} all-to-all(bf16[32,8,128]{2,1,0:T(8,128)(2,1)S(1)} %shard_map.68), channel_id=1, replica_groups=mesh['chip'=32,'core'=2,'mesh'=4] {'chip'}, dimensions={0} | all-to-all | bytes 131072 | tf_op jit(solution)/shard_map/all_to_all | solution.py:251
  53.6 0.6 %shard_map.69 = bf16[5,32,96]{2,1,0:T(8,128)(2,1)} custom-call(bf16[32,8,128]{2,1,0:T(8,128)(2,1)S(1)} %all_to_all.10.got_ref), custom_call_target="tpu_custom_call" | custom-call | tf_op jit(solution)/shard_map/pallas_call | solution.py:252
  (1 shorter events, 0.0 us)
Async XLA Ops:
  0.0 32.4 %copy-start = (bf16[11,48,6,96]{3,1,2,0:T(8,128)(2,1)S(1)}, bf16[11,48,6,96]{3,1,2,0:T(8,128)(2,1)}, u32[]{:S(2)}) copy-start(bf16[11,48,6,96]{3,1,2,0:T(8,128)(2,1)} %param.7) | copy-start | bytes 1824772
  0.0 6.4 %collective-permute-start = (bf16[5,32,96]{2,1,0:T(8,128)(2,1)}, bf16[5,32,96]{2,1,0:T(8,128)(2,1)S(1)}, u32[]{:S(2)}, u32[]{:S(2)}) collective-permute-start(bf16[5,32,96]{2,1,0:T(8,128)(2,1)} %bitcast.9), channel_id=1, source_target_pairs={{0,1},{1,2},{2,3},{3,0},{4,7},{5,4},{6,5},{7,6},{8,9},{9,10},{10,1... | collective-permute-start | bytes 92168 | tf_op jit(solution)/shard_map/ppermute | solution.py:197
  3.3 6.2 %collective-permute-start.2 = (bf16[5,32,96]{2,1,0:T(8,128)(2,1)}, bf16[5,32,96]{2,1,0:T(8,128)(2,1)S(1)}, u32[]{:S(2)}, u32[]{:S(2)}) collective-permute-start(bf16[5,32,96]{2,1,0:T(8,128)(2,1)} %bitcast.10), channel_id=1, source_target_pairs={{0,3},{1,0},{2,1},{3,2},{4,5},{5,6},{6,7},{7,4},{8,11},{9,8},{10,9... | collective-permute-start | bytes 92168 | tf_op jit(solution)/shard_map/ppermute | solution.py:197
  3.3 29.1 %collective-permute-start.3 = (bf16[11,6,48,96]{3,2,1,0:T(8,128)(2,1)}, bf16[11,6,48,96]{3,2,1,0:T(8,128)(2,1)S(1)}, u32[]{:S(2)}, u32[]{:S(2)}) collective-permute-start(bf16[11,6,48,96]{3,2,1,0:T(8,128)(2,1)} %bitcast.7), channel_id=1, source_target_pairs={{0,4},{4,0},{1,5},{5,1},{2,6},{6,2},{3,7},{7,3},{8,12},{12,8},{9,1... | collective-permute-start | bytes 1824776 | tf_op jit(solution)/shard_map/ppermute | solution.py:222
  6.4 3.0 %collective-permute-start.1 = (bf16[5,32,96]{2,1,0:T(8,128)(2,1)S(1)}, bf16[5,32,96]{2,1,0:T(8,128)(2,1)S(1)}, u32[]{:S(2)}, u32[]{:S(2)}) collective-permute-start(bf16[5,32,96]{2,1,0:T(8,128)(2,1)S(1)} %collective-permute-done.refs_2_), channel_id=1, source_target_pairs={{0,1},{1,2},{2,3},{3,0},{4,7},{5,4},{6,5},{7,6},{8,9},{9,10},{10,1... | collective-permute-start | bytes 92168 | tf_op jit(solution)/shard_map/ppermute | solution.py:197
  10.7 21.7 %all-to-all-start = ((bf16[32,32,128]{2,1,0:T(8,128)(2,1)}), bf16[32,32,128]{2,1,0:T(8,128)(2,1)S(1)}, u32[]{:S(2)}, u32[]{:S(2)}) async-start(bf16[32,32,128]{2,1,0:T(8,128)(2,1)} %bitcast.4), calls=%async_computation | async-start | bytes 524288 | tf_op jit(solution)/shard_map/all_to_all | solution.py:219
  36.4 5.1 %collective-permute-start.4 = (f32[160,128]{1,0:T(8,128)S(1)}, f32[160,128]{1,0:T(8,128)S(1)}, u32[]{:S(2)}, u32[]{:S(2)}) collective-permute-start(f32[160,128]{1,0:T(8,128)S(1)} %get-tuple-element.26), channel_id=1, source_target_pairs={{0,4},{4,0},{1,5},{5,1},{2,6},{6,2},{3,7},{7,3},{8,12},{12,8},{9,1... | collective-permute-start | bytes 245768 | tf_op jit(solution)/shard_map/ppermute | solution.py:245

commit v5 on v4

--- a/solution.py
+++ b/solution.py
@@ -31,6 +31,8 @@
 
 
 TAIL = 3 * LANES
+PIECES = 5
+KEPT = 1
 NT = (((1,), (1,)), ((), ()))
 
 
@@ -38,7 +40,7 @@
     return lax.broadcasted_iota(jnp.int32, (count, width), 0).astype(F32).astype(BF16)
 
 
-def prepare_kernel(half, near_ref, far_ref, cols_ref, high_ref, low_ref, out_ref, rest_hbm, every_row, weights, rest, sem):
+def prepare_kernel(half, near_ref, far_ref, cols_ref, high_ref, low_ref, out_ref, rest_hbm, kept_ref, every_row, weights, rest, sem):
     modes, pairs = cols_ref.shape
     one, zero = jnp.ones((), BF16), jnp.zeros((), BF16)
     iota = sublane_iota(half, pairs)
@@ -55,6 +57,10 @@
         lines = slice(mode * half, (mode + 1) * half)
         out_ref[lines, : 2 * half] = high
         out_ref[lines, 2 * half :] = low[:, 2 * LANES :]
+        if mode >= modes - KEPT:
+            kept = mode - modes + KEPT
+            kept_ref[kept * half : (kept + 1) * half, :] = low[:, : 2 * LANES]
+            continue
         rest[lines, :] = low[:, : 2 * LANES]
         store = pltpu.make_async_copy(rest.at[lines], rest_hbm.at[lines], sem.at[mode])
         store.start()
@@ -79,7 +85,7 @@
     slots, nodes = columns_ref.shape
     columns = columns_ref[...]
     bits = nodes.bit_length() - 1
-    away = jnp.bitwise_and((me - jnp.right_shift(columns, bits)) * (1 - 2 * core), LANES // nodes - 1)
+    away = jnp.bitwise_and(me - jnp.right_shift(columns, bits), LANES // nodes - 1)
     place = away * nodes + jnp.bitwise_and(columns, nodes - 1)
     table[...] = jnp.zeros_like(table)
     table[:slots, :nodes] = place.astype(F32)
@@ -120,9 +126,18 @@
     out_ref[...] = wide[...].astype(BF16)
 
 
-def apply_kernel(own, where_ref, got_ref, theirs_ref, mine_ref, coupling_ref, rest_hbm, near_ref, far_ref, rest, wide, slotted, stack, sem):
-    load = pltpu.make_async_copy(rest_hbm, rest, sem)
-    load.start()
+def apply_kernel(own, where_ref, got_ref, theirs_ref, mine_ref, coupling_ref, kept_ref, rest_hbm, near_ref, far_ref, rest, wide, slotted, stack, sem):
+    pieces = sem.shape[0]
+    length = rest.shape[0] // pieces
+
+    def load(piece):
+        at = pl.ds(pl.multiple_of(piece * length, 16), length)
+        return pltpu.make_async_copy(rest_hbm.at[at], rest.at[at], sem.at[piece])
+
+    @pl.loop(0, pieces)
+    def _(piece):
+        load(piece).start()
+
     core = where_ref[1]
     parts, unit, _ = got_ref.shape
     modes, slots, rows, block = mine_ref.shape
@@ -148,10 +163,14 @@
     for mode in range(modes):
         lines = slice(mode * half, (mode + 1) * half)
         first += jnp.dot(stack[mode], coupling_ref[lines, :], preferred_element_type=F32)
-    load.wait()
-    for mode in range(modes):
-        lines = slice(mode * half, (mode + 1) * half)
-        second += jnp.dot(stack[mode, : 2 * rows], rest[lines, :], preferred_element_type=F32)
+    for kept in range(KEPT):
+        low = kept_ref[kept * half : (kept + 1) * half, :]
+        second += jnp.dot(stack[modes - KEPT + kept, : 2 * rows], low, preferred_element_type=F32)
+    for piece in range(pieces):
+        load(piece).wait()
+    for mode in range(modes - KEPT):
+        low = rest[mode * half : (mode + 1) * half, :]
+        second += jnp.dot(stack[mode, : 2 * rows], low, preferred_element_type=F32)
     both = first[: 2 * rows] + first[2 * rows :]
     tail = first[: 2 * rows, 2 * half :]
     total = jnp.concatenate([both[:, : 2 * LANES] + second, both[:, 2 * LANES : 2 * half] + tail], axis=1)
@@ -191,14 +210,9 @@
 
     swap = [(0, 1), (1, 0)]
     held = jnp.transpose(coefficients, (2, 0, 1))
-
-    def turn(block, way):
-        ways = [(c * meshes + m, c * meshes + (m + (way if c == 0 else -way)) % meshes) for c in range(2) for m in range(meshes)]
-        return lax.ppermute(block, ("core", "mesh"), ways)
-
-    behind = turn(held, 1)
-    ahead = turn(held, -1)
-    across = turn(behind, 1)
+    around = {}
+    for d in (2, 1, 3):
+        around[d] = lax.ppermute(held, "mesh", [(i, (i + d) % meshes) for i in range(meshes)])
     smem = pl.BlockSpec(memory_space=pltpu.SMEM)
     vmem = pl.BlockSpec(memory_space=pltpu.VMEM)
     hbm = pl.BlockSpec(memory_space=pltpu.HBM)
@@ -215,33 +229,37 @@
         lambda *refs: send_kernel(unit, *refs),
         jax.ShapeDtypeStruct((parts * unit, LANES), BF16),
         [pltpu.VMEM((own, LANES, LANES), BF16), pltpu.VMEM((parts * unit, LANES), F32)],
-    )(select, held, behind, across, ahead)
+    )(select, held, *(around[d] for d in (1, 2, 3)))
     got = lax.all_to_all(outgoing.reshape(parts, unit, LANES), "chip", 0, 0, tiled=True)
 
     mine = jnp.transpose(stiffness, (0, 2, 1, 3))
     theirs = lax.ppermute(mine, "core", swap)
-    coupling, rest = call(
+    coupling, rest, kept = call(
         lambda *refs: prepare_kernel(half, *refs),
-        [jax.ShapeDtypeStruct((modes * half, TAIL), BF16), pltpu.HBM((modes * half, 2 * LANES), BF16)],
+        [
+            jax.ShapeDtypeStruct((modes * half, TAIL), BF16),
+            pltpu.HBM(((modes - KEPT) * half, 2 * LANES), BF16),
+            jax.ShapeDtypeStruct((KEPT * half, 2 * LANES), BF16),
+        ],
         [
             *[pltpu.VMEM((2, 2 * half, pairs), BF16)] * 2,
-            pltpu.VMEM((modes * half, 2 * LANES), BF16),
-            pltpu.SemaphoreType.DMA((modes,)),
+            pltpu.VMEM(((modes - KEPT) * half, 2 * LANES), BF16),
+            pltpu.SemaphoreType.DMA((modes - KEPT,)),
         ],
-        out_specs=[vmem, hbm],
+        out_specs=[vmem, hbm, vmem],
     )(*tables)
     partial, other = call(
         lambda *refs: apply_kernel(own, *refs),
         [jax.ShapeDtypeStruct((half, LANES), F32)] * 2,
         [
-            pltpu.VMEM((modes * half, 2 * LANES), BF16),
+            pltpu.VMEM(((modes - KEPT) * half, 2 * LANES), BF16),
             pltpu.VMEM((parts * unit + 8, LANES), F32),
             pltpu.VMEM((slots, half + 8, LANES), F32),
             pltpu.VMEM((modes, 4 * rows, half), BF16),
-            pltpu.SemaphoreType.DMA,
+            pltpu.SemaphoreType.DMA((PIECES,)),
         ],
-        in_specs=[smem] + [vmem] * 4 + [hbm],
-    )(where, got, theirs, mine, coupling, in_hbm(rest))
+        in_specs=[smem] + [vmem] * 5 + [hbm],
+    )(where, got, theirs, mine, coupling, kept, in_hbm(rest))
     other = lax.ppermute(other, "core", swap)
     finished = call(
         lambda *refs: finish_kernel(own, *refs),

time: 54.5 us -> 52.6 us (0.965)
  starting transfers between devices: 22.9 us -> 20.9 us
  Pallas kernels: 13.2 us -> 11.9 us
  waiting for transfers between devices: 5.84 us -> 7.02 us
    ppermute x1, starting transfers between devices: 4.17 us -> 2.54 us  [compute(): other = lax.ppermute(other, 'core', swap)]
    ppermute x1, starting transfers between devices: 3.14 us -> 1.52 us  [compute(): theirs = lax.ppermute(mine, 'core', swap)]
    ppermute x3, starting transfers between devices: 4.43 us -> 5.63 us  [compute(): lax.ppermute(held, 'mesh', [(i, (i + d) % meshes) for i in range(meshes)])]
    all_to_all x1, waiting for transfers between devices: 4.91 us -> 6.09 us  [compute(): lax.all_to_all(outgoing.reshape(parts, unit, LANES), 'chip', 0, 0, tiled=...]
    pallas_call x1, Pallas kernels: 3.98 us -> 3.09 us  [compute(): call(lambda *refs: apply_kernel(own, *refs), [jax.ShapeDtypeStruct((half,...]
where the time goes in v5:
time: 52.6 us; the launch traced here: 52.4 us
  starting transfers between devices  20.9 us (40%)
  blocking collectives  12.4 us (24%)
  Pallas kernels  11.9 us (23%)
  waiting for transfers between devices  7.02 us (13%)
    all_to_all x1, blocking collectives, compute(): returned = lax.all_to_all(finished, 'chip', 0, 0, tiled=True)  12.4 us
    all_to_all x1, starting transfers between devices, compute(): lax.all_to_all(outgoing.reshape(parts, unit, LANES), 'chip', 0, 0, tiled=...  11.2 us
    all_to_all x1, waiting for transfers between devices, compute(): lax.all_to_all(outgoing.reshape(parts, unit, LANES), 'chip', 0, 0, tiled=...  6.09 us
    ppermute x3, starting transfers between devices, compute(): lax.ppermute(held, 'mesh', [(i, (i + d) % meshes) for i in range(meshes)])  5.63 us
    pallas_call x1, Pallas kernels, compute(): call(lambda *refs: prepare_kernel(half, *refs), [jax.ShapeDtypeStruct((mo...  5.09 us
    pallas_call x1, Pallas kernels, compute(): call(lambda *refs: apply_kernel(own, *refs), [jax.ShapeDtypeStruct((half,...  3.09 us
    ppermute x1, starting transfers between devices, compute(): other = lax.ppermute(other, 'core', swap)  2.54 us
    pallas_call x1, Pallas kernels, compute(): call(lambda *refs: tables_kernel(own, *refs), [jax.ShapeDtypeStruct(held....  1.79 us
  transfers between devices with their start and end apart: 6, of which 2 were waited for; matrix products, arithmetic and copies ran while one was open for 0% of the time, Pallas kernels for 16%

profile of v5, /device:TPU:1, one launch (start us, length us, event | category | flops | bytes accessed | tf_op | source)
XLA Modules:
  0.0 52.4 jit_solution(4066944630883290385)
XLA Ops:
  0.0 0.0 copy-start
  0.0 2.0 %collective-permute-start = (bf16[5,32,96]{2,1,0:T(8,128)(2,1)}, bf16[5,32,96]{2,1,0:T(8,128)(2,1)S(1)}, u32[]{:S(2)}, u32[]{:S(2)}) collective-permute-start(bf16[5,32,96]{2,1,0:T(8,128)(2,1)} %bitcast.9), channel_id=1, source_target_pairs={{0,1},{1,2},{2,3},{3,0},{4,5},{5,6},{6,7},{7,4},{8,9},{9,10},{10,1... | collective-permute-start | bytes 92168 | tf_op jit(solution)/shard_map/ppermute | solution.py:215
  2.0 2.5 %collective-permute-start.1 = (bf16[5,32,96]{2,1,0:T(8,128)(2,1)}, bf16[5,32,96]{2,1,0:T(8,128)(2,1)S(1)}, u32[]{:S(2)}, u32[]{:S(2)}) collective-permute-start(bf16[5,32,96]{2,1,0:T(8,128)(2,1)} %bitcast.10), channel_id=1, source_target_pairs={{0,2},{1,3},{2,0},{3,1},{4,6},{5,7},{6,4},{7,5},{8,10},{9,11},{10,... | collective-permute-start | bytes 92168 | tf_op jit(solution)/shard_map/ppermute | solution.py:215
  4.5 1.2 %collective-permute-start.2 = (bf16[5,32,96]{2,1,0:T(8,128)(2,1)}, bf16[5,32,96]{2,1,0:T(8,128)(2,1)S(1)}, u32[]{:S(2)}, u32[]{:S(2)}) collective-permute-start(bf16[5,32,96]{2,1,0:T(8,128)(2,1)} %bitcast.11), channel_id=1, source_target_pairs={{0,3},{1,0},{2,1},{3,2},{4,7},{5,4},{6,5},{7,6},{8,11},{9,8},{10,9... | collective-permute-start | bytes 92168 | tf_op jit(solution)/shard_map/ppermute | solution.py:215
  5.6 1.5 %collective-permute-start.3 = (bf16[11,6,48,96]{3,2,1,0:T(8,128)(2,1)}, bf16[11,6,48,96]{3,2,1,0:T(8,128)(2,1)S(1)}, u32[]{:S(2)}, u32[]{:S(2)}) collective-permute-start(bf16[11,6,48,96]{3,2,1,0:T(8,128)(2,1)} %bitcast.7), channel_id=1, source_target_pairs={{0,4},{4,0},{1,5},{5,1},{2,6},{6,2},{3,7},{7,3},{8,12},{12,8},{9,1... | collective-permute-start | bytes 1824776 | tf_op jit(solution)/shard_map/ppermute | solution.py:236
  7.2 0.1 pad_add_fusion.refs_0_
  7.2 1.8 %shard_map.64 = (bf16[5,32,96]{2,1,0:T(8,128)(2,1)S(1)}, bf16[192,128]{1,0:T(8,128)(2,1)S(1)}, bf16[11,1280]{1,0:T(8,128)(2,1)S(1)}, bf16[11,1280]{1,0:T(8,128)(...) custom-call(s32[2]{0:T(128)S(1)} %pad_add_fusion.refs_0_, ...), custom_call_target="tpu_custom_call" | custom-call | tf_op jit(solution)/shard_map/pallas_call | solution.py:220
  9.0 0.0 collective-permute-done.refs_2_
  9.0 0.0 collective-permute-done.1.refs_3_
  9.1 0.0 collective-permute-done.2.refs_4_
  9.1 1.2 %shard_map.65 = bf16[1024,128]{1,0:T(8,128)(2,1)} custom-call(bf16[192,128]{1,0:T(8,128)(2,1)S(1)} %get-tuple-element.17.refs_0_, bf16[5,32,96]{2,1,0:T(8,128)(2,1)S(1)} %get-tuple-element.18.refs_1_, bf16[5,32,96]{2,1,0:T(8,128)(2,1)S(1)} %collective-permute-done.refs_2_, bf16[5,32,96]{2,1,0:T(8,128)(2,1)S(1)} %collective-permute-done.1.refs_3_, ...), custom_call_target="tpu_custom_call" | custom-call | tf_op jit(solution)/shard_map/pallas_call | solution.py:228
  10.3 11.2 %all-to-all-start = ((bf16[32,32,128]{2,1,0:T(8,128)(2,1)}), bf16[32,32,128]{2,1,0:T(8,128)(2,1)S(1)}, u32[]{:S(2)}, u32[]{:S(2)}) async-start(bf16[32,32,128]{2,1,0:T(8,128)(2,1)} %bitcast.4), calls=%async_computation | async-start | bytes 524288 | tf_op jit(solution)/shard_map/all_to_all | solution.py:233
  21.5 5.1 %shard_map.66 = (bf16[1760,384]{1,0:T(8,128)(2,1)S(1)}, bf16[1600,256]{1,0:T(8,128)(2,1)}, bf16[160,256]{1,0:T(8,128)(2,1)S(1)}) custom-call(bf16[11,1280]{1,0:T(8,128)(2,1)S(1)} %get-tuple-element.19.refs_0_, bf16[11,1280]{1,0:T(8,128)(2,1)S(1)} %get-tuple-element.20.refs_1_, bf16[11,1280]{1,0:T(8,128)(2,1)S(1)} %get-tuple-element.21.refs_2_, ...), custom_call_target="tpu_custom_call" | custom-call | tf_op jit(solution)/shard_map/pallas_call | solution.py:237
  26.6 6.1 %all-to-all-done.refs_1_ = bf16[32,32,128]{2,1,0:T(8,128)(2,1)S(1)} async-done(((bf16[32,32,128]{2,1,0:T(8,128)(2,1)}), bf16[32,32,128]{2,1,0:T(8,128)(2,1)S(1)}, u32[]{:S(2)}, u32[]{:S(2)}) %all-to-all-start) | async-done | bytes 262176 | tf_op jit(solution)/shard_map/all_to_all | solution.py:233
  32.7 0.0 collective-permute-done.3.refs_2_
  32.7 0.0 copy-done
  32.7 3.1 %shard_map.67 = (f32[160,128]{1,0:T(8,128)S(1)}, f32[160,128]{1,0:T(8,128)S(1)}) custom-call(s32[2]{0:T(128)S(1)} %pad_add_fusion.refs_0_, bf16[32,32,128]{2,1,0:T(8,128)(2,1)S(1)} %all-to-all-done.refs_1_, bf16[11,6,48,96]{3,2,1,0:T(8,128)(2,1)S(1)} %collective-permute-done.3.refs_2_, bf16[11,6,48,96]{3,2,1,0:T(8,128)(2,1)S(1)} %bitcast.8, ...), custom_call_target="tpu_custom_call" | custom-call | tf_op jit(solution)/shard_map/pallas_call | solution.py:251
  35.8 2.5 %collective-permute-start.4 = (f32[160,128]{1,0:T(8,128)S(1)}, f32[160,128]{1,0:T(8,128)S(1)}, u32[]{:S(2)}, u32[]{:S(2)}) collective-permute-start(f32[160,128]{1,0:T(8,128)S(1)} %get-tuple-element.28), channel_id=1, source_target_pairs={{0,4},{4,0},{1,5},{5,1},{2,6},{6,2},{3,7},{7,3},{8,12},{12,8},{9,1... | collective-permute-start | bytes 245768 | tf_op jit(solution)/shard_map/ppermute | solution.py:263
  38.3 0.9 %collective-permute-done.4.refs_1_ = f32[160,128]{1,0:T(8,128)S(1)} collective-permute-done((f32[160,128]{1,0:T(8,128)S(1)}, f32[160,128]{1,0:T(8,128)S(1)}, u32[]{:S(2)}, u32[]{:S(2)}) %collective-permute-start.4) | collective-permute-done | bytes 81952 | tf_op jit(solution)/shard_map/ppermute | solution.py:263
  39.3 12.4 %all_to_all.10.got_ref = bf16[32,8,128]{2,1,0:T(8,128)(2,1)S(1)} all-to-all(bf16[32,8,128]{2,1,0:T(8,128)(2,1)S(1)} %shard_map.68), channel_id=1, replica_groups=mesh['chip'=32,'core'=2,'mesh'=4] {'chip'}, dimensions={0} | all-to-all | bytes 131072 | tf_op jit(solution)/shard_map/all_to_all | solution.py:269
  51.7 0.6 %shard_map.69 = bf16[5,32,96]{2,1,0:T(8,128)(2,1)} custom-call(bf16[32,8,128]{2,1,0:T(8,128)(2,1)S(1)} %all_to_all.10.got_ref), custom_call_target="tpu_custom_call" | custom-call | tf_op jit(solution)/shard_map/pallas_call | solution.py:270
  (1 shorter events, 0.0 us)
Async XLA Ops:
  0.0 32.7 %copy-start = (bf16[11,48,6,96]{3,1,2,0:T(8,128)(2,1)S(1)}, bf16[11,48,6,96]{3,1,2,0:T(8,128)(2,1)}, u32[]{:S(2)}) copy-start(bf16[11,48,6,96]{3,1,2,0:T(8,128)(2,1)} %param.7) | copy-start | bytes 1824772
  0.0 9.0 %collective-permute-start = (bf16[5,32,96]{2,1,0:T(8,128)(2,1)}, bf16[5,32,96]{2,1,0:T(8,128)(2,1)S(1)}, u32[]{:S(2)}, u32[]{:S(2)}) collective-permute-start(bf16[5,32,96]{2,1,0:T(8,128)(2,1)} %bitcast.9), channel_id=1, source_target_pairs={{0,1},{1,2},{2,3},{3,0},{4,5},{5,6},{6,7},{7,4},{8,9},{9,10},{10,1... | collective-permute-start | bytes 92168 | tf_op jit(solution)/shard_map/ppermute | solution.py:215
  2.0 7.0 %collective-permute-start.1 = (bf16[5,32,96]{2,1,0:T(8,128)(2,1)}, bf16[5,32,96]{2,1,0:T(8,128)(2,1)S(1)}, u32[]{:S(2)}, u32[]{:S(2)}) collective-permute-start(bf16[5,32,96]{2,1,0:T(8,128)(2,1)} %bitcast.10), channel_id=1, source_target_pairs={{0,2},{1,3},{2,0},{3,1},{4,6},{5,7},{6,4},{7,5},{8,10},{9,11},{10,... | collective-permute-start | bytes 92168 | tf_op jit(solution)/shard_map/ppermute | solution.py:215
  4.5 4.6 %collective-permute-start.2 = (bf16[5,32,96]{2,1,0:T(8,128)(2,1)}, bf16[5,32,96]{2,1,0:T(8,128)(2,1)S(1)}, u32[]{:S(2)}, u32[]{:S(2)}) collective-permute-start(bf16[5,32,96]{2,1,0:T(8,128)(2,1)} %bitcast.11), channel_id=1, source_target_pairs={{0,3},{1,0},{2,1},{3,2},{4,7},{5,4},{6,5},{7,6},{8,11},{9,8},{10,9... | collective-permute-start | bytes 92168 | tf_op jit(solution)/shard_map/ppermute | solution.py:215
  5.6 27.1 %collective-permute-start.3 = (bf16[11,6,48,96]{3,2,1,0:T(8,128)(2,1)}, bf16[11,6,48,96]{3,2,1,0:T(8,128)(2,1)S(1)}, u32[]{:S(2)}, u32[]{:S(2)}) collective-permute-start(bf16[11,6,48,96]{3,2,1,0:T(8,128)(2,1)} %bitcast.7), channel_id=1, source_target_pairs={{0,4},{4,0},{1,5},{5,1},{2,6},{6,2},{3,7},{7,3},{8,12},{12,8},{9,1... | collective-permute-start | bytes 1824776 | tf_op jit(solution)/shard_map/ppermute | solution.py:236
  10.3 22.4 %all-to-all-start = ((bf16[32,32,128]{2,1,0:T(8,128)(2,1)}), bf16[32,32,128]{2,1,0:T(8,128)(2,1)S(1)}, u32[]{:S(2)}, u32[]{:S(2)}) async-start(bf16[32,32,128]{2,1,0:T(8,128)(2,1)} %bitcast.4), calls=%async_computation | async-start | bytes 524288 | tf_op jit(solution)/shard_map/all_to_all | solution.py:233
  35.8 3.5 %collective-permute-start.4 = (f32[160,128]{1,0:T(8,128)S(1)}, f32[160,128]{1,0:T(8,128)S(1)}, u32[]{:S(2)}, u32[]{:S(2)}) collective-permute-start(f32[160,128]{1,0:T(8,128)S(1)} %get-tuple-element.28), channel_id=1, source_target_pairs={{0,4},{4,0},{1,5},{5,1},{2,6},{6,2},{3,7},{7,3},{8,12},{12,8},{9,1... | collective-permute-start | bytes 245768 | tf_op jit(solution)/shard_map/ppermute | solution.py:263

commit v6 on v5

--- a/solution.py
+++ b/solution.py
@@ -69,7 +69,7 @@
         store.wait()
 
 
-def tables_kernel(own, where_ref, *refs):
+def tables_kernel(own, *refs):
     (held_hbm, *tables_hbm), (held_ref, out_ref, near_ref, far_ref, at_ref, high_ref, low_ref) = refs[:5], refs[5:12]
     columns_ref, rows_ref, cols_ref, vals_ref, table, sem = refs[12:]
     targets = (columns_ref, rows_ref, cols_ref, vals_ref, held_ref)
@@ -81,7 +81,7 @@
         load.start()
     for load in loads:
         load.wait()
-    me, core = where_ref[0], where_ref[1]
+    me, core = lax.axis_index("mesh"), lax.axis_index("core")
     slots, nodes = columns_ref.shape
     columns = columns_ref[...]
     bits = nodes.bit_length() - 1
@@ -126,7 +126,7 @@
     out_ref[...] = wide[...].astype(BF16)
 
 
-def apply_kernel(own, where_ref, got_ref, theirs_ref, mine_ref, coupling_ref, kept_ref, rest_hbm, near_ref, far_ref, rest, wide, slotted, stack, sem):
+def apply_kernel(own, got_ref, theirs_ref, mine_ref, coupling_ref, kept_ref, rest_hbm, near_ref, far_ref, rest, wide, slotted, stack, sem):
     pieces = sem.shape[0]
     length = rest.shape[0] // pieces
 
@@ -138,7 +138,7 @@
     def _(piece):
         load(piece).start()
 
-    core = where_ref[1]
+    core = lax.axis_index("core")
     parts, unit, _ = got_ref.shape
     modes, slots, rows, block = mine_ref.shape
     half = own * parts
@@ -206,14 +206,12 @@
     meshes = lax.axis_size("mesh")
     half = own * parts
     unit = 32
-    where = jnp.stack([lax.axis_index("mesh"), lax.axis_index("core")]).astype(jnp.int32)
 
     swap = [(0, 1), (1, 0)]
     held = jnp.transpose(coefficients, (2, 0, 1))
     around = {}
     for d in (2, 1, 3):
         around[d] = lax.ppermute(held, "mesh", [(i, (i + d) % meshes) for i in range(meshes)])
-    smem = pl.BlockSpec(memory_space=pltpu.SMEM)
     vmem = pl.BlockSpec(memory_space=pltpu.VMEM)
     hbm = pl.BlockSpec(memory_space=pltpu.HBM)
     entries = jax.ShapeDtypeStruct((modes, pairs), BF16)
@@ -223,8 +221,8 @@
         [pltpu.VMEM((slots, nodes), jnp.int32)]
         + [pltpu.VMEM((modes, pairs), x.dtype) for x in (pair_rows, pair_cols, pair_vals)]
         + [pltpu.VMEM((8, LANES), F32), pltpu.SemaphoreType.DMA((5,))],
-        in_specs=[smem] + [hbm] * 5,
-    )(where, *map(in_hbm, (held, columns.T, pair_rows, pair_cols, pair_vals)))
+        in_specs=[hbm] * 5,
+    )(*map(in_hbm, (held, columns.T, pair_rows, pair_cols, pair_vals)))
     outgoing = call(
         lambda *refs: send_kernel(unit, *refs),
         jax.ShapeDtypeStruct((parts * unit, LANES), BF16),
@@ -258,8 +256,8 @@
             pltpu.VMEM((modes, 4 * rows, half), BF16),
             pltpu.SemaphoreType.DMA((PIECES,)),
         ],
-        in_specs=[smem] + [vmem] * 5 + [hbm],
-    )(where, got, theirs, mine, coupling, kept, in_hbm(rest))
+        in_specs=[vmem] * 5 + [hbm],
+    )(got, theirs, mine, coupling, kept, in_hbm(rest))
     other = lax.ppermute(other, "core", swap)
     finished = call(
         lambda *refs: finish_kernel(own, *refs),

time: 52.6 us -> 51.4 us (0.977)
  Pallas kernels: 11.9 us -> 10.7 us
  waiting for transfers between devices: 7.02 us -> 7.57 us
    ppermute x3, starting transfers between devices: 5.63 us -> 3.11 us  [compute(): lax.ppermute(held, 'mesh', [(i, (i + d) % meshes) for i in range(meshes)])]
    ppermute x1, starting transfers between devices: 1.52 us -> 3.2 us  [compute(): theirs = lax.ppermute(mine, 'core', swap)]
    ppermute x3, waiting for transfers between devices: 0.01 us -> 1.34 us  [compute(): lax.ppermute(held, 'mesh', [(i, (i + d) % meshes) for i in range(meshes)])]
    ppermute x1, starting transfers between devices: 2.54 us -> 3.86 us  [compute(): other = lax.ppermute(other, 'core', swap)]
    all_to_all x1, waiting for transfers between devices: 6.09 us -> 5.3 us  [compute(): lax.all_to_all(outgoing.reshape(parts, unit, LANES), 'chip', 0, 0, tiled=...]
    pallas_call x1, Pallas kernels: 3.09 us -> 2.46 us  [compute(): call(lambda *refs: apply_kernel(own, *refs), [jax.ShapeDtypeStruct((half,...]
    pallas_call x1, Pallas kernels: 1.79 us -> 1.26 us  [compute(): call(lambda *refs: tables_kernel(own, *refs), [jax.ShapeDtypeStruct(held....]
  transfers between devices with their start and end apart: 6 -> 6, of which waited for: 2 -> 4; matrix products, arithmetic and copies ran while one was open for 0% -> 0% of each run, Pallas kernels for 16% -> 15%
where the time goes in v6:
time: 51.4 us; the launch traced here: 51.1 us
  starting transfers between devices  20.9 us (41%)
  blocking collectives  11.9 us (23%)
  Pallas kernels  10.7 us (21%)
  waiting for transfers between devices  7.57 us (15%)
    all_to_all x1, blocking collectives, compute(): returned = lax.all_to_all(finished, 'chip', 0, 0, tiled=True)  11.9 us
    all_to_all x1, starting transfers between devices, compute(): lax.all_to_all(outgoing.reshape(parts, unit, LANES), 'chip', 0, 0, tiled=...  10.7 us
    all_to_all x1, waiting for transfers between devices, compute(): lax.all_to_all(outgoing.reshape(parts, unit, LANES), 'chip', 0, 0, tiled=...  5.3 us
    pallas_call x1, Pallas kernels, compute(): call(lambda *refs: prepare_kernel(half, *refs), [jax.ShapeDtypeStruct((mo...  5.09 us
    ppermute x1, starting transfers between devices, compute(): other = lax.ppermute(other, 'core', swap)  3.86 us
    ppermute x1, starting transfers between devices, compute(): theirs = lax.ppermute(mine, 'core', swap)  3.2 us
    ppermute x3, starting transfers between devices, compute(): lax.ppermute(held, 'mesh', [(i, (i + d) % meshes) for i in range(meshes)])  3.11 us
    pallas_call x1, Pallas kernels, compute(): call(lambda *refs: apply_kernel(own, *refs), [jax.ShapeDtypeStruct((half,...  2.46 us
  transfers between devices with their start and end apart: 6, of which 4 were waited for; matrix products, arithmetic and copies ran while one was open for 0% of the time, Pallas kernels for 15%

profile of v6, /device:TPU:1, one launch (start us, length us, event | category | flops | bytes accessed | tf_op | source)
XLA Modules:
  0.0 51.1 jit_solution(4566763040603466906)
XLA Ops:
  0.0 0.0 copy-start
  0.0 3.2 %collective-permute-start.3 = (bf16[11,6,48,96]{3,2,1,0:T(8,128)(2,1)}, bf16[11,6,48,96]{3,2,1,0:T(8,128)(2,1)S(1)}, u32[]{:S(2)}, u32[]{:S(2)}) collective-permute-start(bf16[11,6,48,96]{3,2,1,0:T(8,128)(2,1)} %bitcast.5), channel_id=1, source_target_pairs={{0,4},{4,0},{1,5},{5,1},{2,6},{6,2},{3,7},{7,3},{8,12},{12,8},{9,1... | collective-permute-start | bytes 1824776 | tf_op jit(solution)/shard_map/ppermute | solution.py:234
  3.2 0.0 collective-permute-start
  3.2 2.0 %collective-permute-start.1 = (bf16[5,32,96]{2,1,0:T(8,128)(2,1)}, bf16[5,32,96]{2,1,0:T(8,128)(2,1)S(1)}, u32[]{:S(2)}, u32[]{:S(2)}) collective-permute-start(bf16[5,32,96]{2,1,0:T(8,128)(2,1)} %bitcast.8), channel_id=1, source_target_pairs={{0,2},{1,3},{2,0},{3,1},{4,6},{5,7},{6,4},{7,5},{8,10},{9,11},{10,... | collective-permute-start | bytes 92168 | tf_op jit(solution)/shard_map/ppermute | solution.py:214
  5.2 1.2 %collective-permute-start.2 = (bf16[5,32,96]{2,1,0:T(8,128)(2,1)}, bf16[5,32,96]{2,1,0:T(8,128)(2,1)S(1)}, u32[]{:S(2)}, u32[]{:S(2)}) collective-permute-start(bf16[5,32,96]{2,1,0:T(8,128)(2,1)} %bitcast.9), channel_id=1, source_target_pairs={{0,3},{1,0},{2,1},{3,2},{4,7},{5,4},{6,5},{7,6},{8,11},{9,8},{10,9... | collective-permute-start | bytes 92168 | tf_op jit(solution)/shard_map/ppermute | solution.py:214
  6.3 1.3 %shard_map.64 = (bf16[5,32,96]{2,1,0:T(8,128)(2,1)S(1)}, bf16[192,128]{1,0:T(8,128)(2,1)S(1)}, bf16[11,1280]{1,0:T(8,128)(2,1)S(1)}, bf16[11,1280]{1,0:T(8,128)(...) custom-call(bf16[5,32,96]{2,1,0:T(8,128)(2,1)} %bitcast.10, ...), custom_call_target="tpu_custom_call" | custom-call | tf_op jit(solution)/shard_map/pallas_call | solution.py:218
  7.6 1.1 %collective-permute-done.refs_2_ = bf16[5,32,96]{2,1,0:T(8,128)(2,1)S(1)} collective-permute-done((bf16[5,32,96]{2,1,0:T(8,128)(2,1)}, bf16[5,32,96]{2,1,0:T(8,128)(2,1)S(1)}, u32[]{:S(2)}, u32[]{:S(2)}) %collective-permute-start) | collective-permute-done | bytes 30752 | tf_op jit(solution)/shard_map/ppermute | solution.py:214
  8.7 0.0 collective-permute-done.1.refs_3_
  8.7 0.2 collective-permute-done.2.refs_4_
  8.9 1.2 %shard_map.65 = bf16[1024,128]{1,0:T(8,128)(2,1)} custom-call(bf16[192,128]{1,0:T(8,128)(2,1)S(1)} %get-tuple-element.17.refs_0_, bf16[5,32,96]{2,1,0:T(8,128)(2,1)S(1)} %get-tuple-element.18.refs_1_, bf16[5,32,96]{2,1,0:T(8,128)(2,1)S(1)} %collective-permute-done.refs_2_, bf16[5,32,96]{2,1,0:T(8,128)(2,1)S(1)} %collective-permute-done.1.refs_3_, ...), custom_call_target="tpu_custom_call" | custom-call | tf_op jit(solution)/shard_map/pallas_call | solution.py:226
  10.2 10.7 %all-to-all-start = ((bf16[32,32,128]{2,1,0:T(8,128)(2,1)}), bf16[32,32,128]{2,1,0:T(8,128)(2,1)S(1)}, u32[]{:S(2)}, u32[]{:S(2)}) async-start(bf16[32,32,128]{2,1,0:T(8,128)(2,1)} %bitcast.2), calls=%async_computation | async-start | bytes 524288 | tf_op jit(solution)/shard_map/all_to_all | solution.py:231
  20.9 5.1 %shard_map.66 = (bf16[1760,384]{1,0:T(8,128)(2,1)S(1)}, bf16[1600,256]{1,0:T(8,128)(2,1)}, bf16[160,256]{1,0:T(8,128)(2,1)S(1)}) custom-call(bf16[11,1280]{1,0:T(8,128)(2,1)S(1)} %get-tuple-element.19.refs_0_, bf16[11,1280]{1,0:T(8,128)(2,1)S(1)} %get-tuple-element.20.refs_1_, bf16[11,1280]{1,0:T(8,128)(2,1)S(1)} %get-tuple-element.21.refs_2_, ...), custom_call_target="tpu_custom_call" | custom-call | tf_op jit(solution)/shard_map/pallas_call | solution.py:235
  26.0 5.3 %all-to-all-done.refs_0_ = bf16[32,32,128]{2,1,0:T(8,128)(2,1)S(1)} async-done(((bf16[32,32,128]{2,1,0:T(8,128)(2,1)}), bf16[32,32,128]{2,1,0:T(8,128)(2,1)S(1)}, u32[]{:S(2)}, u32[]{:S(2)}) %all-to-all-start) | async-done | bytes 262176 | tf_op jit(solution)/shard_map/all_to_all | solution.py:231
  31.3 0.0 collective-permute-done.3.refs_1_
  31.3 0.0 copy-done
  31.3 2.5 %shard_map.67 = (f32[160,128]{1,0:T(8,128)S(1)}, f32[160,128]{1,0:T(8,128)S(1)}) custom-call(bf16[32,32,128]{2,1,0:T(8,128)(2,1)S(1)} %all-to-all-done.refs_0_, bf16[11,6,48,96]{3,2,1,0:T(8,128)(2,1)S(1)} %collective-permute-done.3.refs_1_, bf16[11,6,48,96]{3,2,1,0:T(8,128)(2,1)S(1)} %bitcast.6, bf16[1760,384]{1,0:T(8,128)(2,1)S(1)} %get-tuple-element.24.refs_3_, ...), custom_call_target="tpu_custom_call" | custom-call | tf_op jit(solution)/shard_map/pallas_call | solution.py:249
  33.8 3.9 %collective-permute-start.4 = (f32[160,128]{1,0:T(8,128)S(1)}, f32[160,128]{1,0:T(8,128)S(1)}, u32[]{:S(2)}, u32[]{:S(2)}) collective-permute-start(f32[160,128]{1,0:T(8,128)S(1)} %get-tuple-element.28), channel_id=1, source_target_pairs={{0,4},{4,0},{1,5},{5,1},{2,6},{6,2},{3,7},{7,3},{8,12},{12,8},{9,1... | collective-permute-start | bytes 245768 | tf_op jit(solution)/shard_map/ppermute | solution.py:261
  37.6 0.9 %collective-permute-done.4.refs_1_ = f32[160,128]{1,0:T(8,128)S(1)} collective-permute-done((f32[160,128]{1,0:T(8,128)S(1)}, f32[160,128]{1,0:T(8,128)S(1)}, u32[]{:S(2)}, u32[]{:S(2)}) %collective-permute-start.4) | collective-permute-done | bytes 81952 | tf_op jit(solution)/shard_map/ppermute | solution.py:261
  38.6 11.9 %all_to_all.10.got_ref = bf16[32,8,128]{2,1,0:T(8,128)(2,1)S(1)} all-to-all(bf16[32,8,128]{2,1,0:T(8,128)(2,1)S(1)} %shard_map.68), channel_id=1, replica_groups=mesh['chip'=32,'core'=2,'mesh'=4] {'chip'}, dimensions={0} | all-to-all | bytes 131072 | tf_op jit(solution)/shard_map/all_to_all | solution.py:267
  50.5 0.6 %shard_map.69 = bf16[5,32,96]{2,1,0:T(8,128)(2,1)} custom-call(bf16[32,8,128]{2,1,0:T(8,128)(2,1)S(1)} %all_to_all.10.got_ref), custom_call_target="tpu_custom_call" | custom-call | tf_op jit(solution)/shard_map/pallas_call | solution.py:268
  (1 shorter events, 0.0 us)
Async XLA Ops:
  0.0 31.3 %copy-start = (bf16[11,48,6,96]{3,1,2,0:T(8,128)(2,1)S(1)}, bf16[11,48,6,96]{3,1,2,0:T(8,128)(2,1)}, u32[]{:S(2)}) copy-start(bf16[11,48,6,96]{3,1,2,0:T(8,128)(2,1)} %param.7) | copy-start | bytes 1824772
  0.0 31.3 %collective-permute-start.3 = (bf16[11,6,48,96]{3,2,1,0:T(8,128)(2,1)}, bf16[11,6,48,96]{3,2,1,0:T(8,128)(2,1)S(1)}, u32[]{:S(2)}, u32[]{:S(2)}) collective-permute-start(bf16[11,6,48,96]{3,2,1,0:T(8,128)(2,1)} %bitcast.5), channel_id=1, source_target_pairs={{0,4},{4,0},{1,5},{5,1},{2,6},{6,2},{3,7},{7,3},{8,12},{12,8},{9,1... | collective-permute-start | bytes 1824776 | tf_op jit(solution)/shard_map/ppermute | solution.py:234
  3.2 5.5 %collective-permute-start = (bf16[5,32,96]{2,1,0:T(8,128)(2,1)}, bf16[5,32,96]{2,1,0:T(8,128)(2,1)S(1)}, u32[]{:S(2)}, u32[]{:S(2)}) collective-permute-start(bf16[5,32,96]{2,1,0:T(8,128)(2,1)} %bitcast.7), channel_id=1, source_target_pairs={{0,1},{1,2},{2,3},{3,0},{4,5},{5,6},{6,7},{7,4},{8,9},{9,10},{10,1... | collective-permute-start | bytes 92168 | tf_op jit(solution)/shard_map/ppermute | solution.py:214
  3.2 5.5 %collective-permute-start.1 = (bf16[5,32,96]{2,1,0:T(8,128)(2,1)}, bf16[5,32,96]{2,1,0:T(8,128)(2,1)S(1)}, u32[]{:S(2)}, u32[]{:S(2)}) collective-permute-start(bf16[5,32,96]{2,1,0:T(8,128)(2,1)} %bitcast.8), channel_id=1, source_target_pairs={{0,2},{1,3},{2,0},{3,1},{4,6},{5,7},{6,4},{7,5},{8,10},{9,11},{10,... | collective-permute-start | bytes 92168 | tf_op jit(solution)/shard_map/ppermute | solution.py:214
  5.2 3.8 %collective-permute-start.2 = (bf16[5,32,96]{2,1,0:T(8,128)(2,1)}, bf16[5,32,96]{2,1,0:T(8,128)(2,1)S(1)}, u32[]{:S(2)}, u32[]{:S(2)}) collective-permute-start(bf16[5,32,96]{2,1,0:T(8,128)(2,1)} %bitcast.9), channel_id=1, source_target_pairs={{0,3},{1,0},{2,1},{3,2},{4,7},{5,4},{6,5},{7,6},{8,11},{9,8},{10,9... | collective-permute-start | bytes 92168 | tf_op jit(solution)/shard_map/ppermute | solution.py:214
  10.2 21.1 %all-to-all-start = ((bf16[32,32,128]{2,1,0:T(8,128)(2,1)}), bf16[32,32,128]{2,1,0:T(8,128)(2,1)S(1)}, u32[]{:S(2)}, u32[]{:S(2)}) async-start(bf16[32,32,128]{2,1,0:T(8,128)(2,1)} %bitcast.2), calls=%async_computation | async-start | bytes 524288 | tf_op jit(solution)/shard_map/all_to_all | solution.py:231
  33.8 4.8 %collective-permute-start.4 = (f32[160,128]{1,0:T(8,128)S(1)}, f32[160,128]{1,0:T(8,128)S(1)}, u32[]{:S(2)}, u32[]{:S(2)}) collective-permute-start(f32[160,128]{1,0:T(8,128)S(1)} %get-tuple-element.28), channel_id=1, source_target_pairs={{0,4},{4,0},{1,5},{5,1},{2,6},{6,2},{3,7},{7,3},{8,12},{12,8},{9,1... | collective-permute-start | bytes 245768 | tf_op jit(solution)/shard_map/ppermute | solution.py:261
